TPU v7x, 256 devices: a whole 4x4x8 slice. The times are simulated.
256 devices in a mesh: dp: 16 (over y_hi, z), fsdp: 16 (over y_lo, x, core).
Axes of the slice: x: 4, y: 4 (y_hi: 2, y_lo: 2; y = y_hi * 2 + y_lo), z: 8, core: 2. Of those that a mesh axis runs over, the one named last changes fastest.
Arguments:
- item_tokens: bfloat16 [131072, 4096], P(('dp', 'fsdp')), may hold values from -6 to 6
- item_lengths: int32 [1024], P(('dp', 'fsdp')), may hold values from 1 to 128
- item_gain: float32 [4096], replicated, may hold values from 0.1 to 1.9
- user_source: int32 [65536, 1], P(('dp', 'fsdp')), may hold values from 0 to 15; in each aligned block of 256 rows (0 to 255, 256 to 511, ...) at most 24 rows name the same one
- user_slot: int32 [65536], P(('dp', 'fsdp')), may hold values from 0 to 3
- user_lengths: int32 [256], P(('dp', 'fsdp')), may hold values from 1 to 256
- user_gain: float32 [4096], replicated, may hold values from 0.1 to 1.9
- key_weight: bfloat16 [4096, 1024], P('fsdp'), may hold values from -0.09375 to 0.09375
- key_grad: bfloat16 [65536, 1024], P(('dp', 'fsdp')), may hold values from -6 to 6
Outputs:
- keys: bfloat16 [65536, 1024], P(('dp', 'fsdp'))
- weight_grad: float32 [4096, 1024], P('fsdp')
- token_grads: bfloat16 [131072, 4096], P(('dp', 'fsdp'))
Inputs may be any that keep to these rules, and one draw needn't show every extreme that they name: `user_source`: among the 256 positions of one device, no source index appears more than 24 times, and in every draw some device reaches 24 for some source.
All inputs are finite; a program needn't handle non-finite values.
Results may differ from a plain program's by a relative error of at most 0.0057.
Values may be sent and summed in bfloat16 or wider, within the bound.
A program may use at most 128 MiB of HBM per device.

v0:
```python
import jax
import jax.numpy as jnp
from jax import lax
from jax.sharding import PartitionSpec as P

EPS = 1e-05


def rms_scale(vector, gain_row):
    return vector * lax.rsqrt(jnp.mean(vector * vector, axis=-1, keepdims=True) + EPS) * gain_row


def pool_items(token_block, valid_mask, item_sizes, gain_row):
    normed = rms_scale(token_block, gain_row)
    return jnp.sum(normed * valid_mask[:, :, None], axis=1) / item_sizes[:, None]


def local(
    item_tokens,
    item_lengths,
    item_gain,
    user_source,
    user_slot,
    user_lengths,
    user_gain,
    key_weight,
    key_grad,
):
    item_count = item_lengths.shape[0]
    block_rows = item_tokens.shape[0] // item_count
    model_width = item_tokens.shape[1]
    group_count = lax.axis_size("dp")
    stacked_tokens = item_tokens.reshape(item_count, block_rows, model_width)
    valid_mask = (
        lax.broadcasted_iota(jnp.int32, (item_count, block_rows), 1) < item_lengths[:, None]
    ).astype(jnp.float32)
    item_sizes = item_lengths.astype(jnp.float32)

    def pooling(tokens_float):
        return pool_items(tokens_float, valid_mask, item_sizes, item_gain)

    pooled, pool_back = jax.vjp(pooling, stacked_tokens.astype(jnp.float32))
    item_emb = pooled.astype(jnp.bfloat16)
    weights = lax.all_gather(key_weight, "fsdp", axis=0, tiled=True)
    row_count = user_slot.shape[0]
    source = user_source[:, 0]
    seq_count = user_lengths.shape[0]
    seq_rows = row_count // seq_count
    alive_mask = (
        lax.broadcasted_iota(jnp.int32, (seq_count, seq_rows), 1) < user_lengths[:, None]
    ).reshape(row_count, 1)
    capacity = 3 * row_count // (2 * group_count)
    source_hot = (
        source[:, None] == lax.broadcasted_iota(jnp.int32, (row_count, group_count), 1)
    ).astype(jnp.int32)
    before = jnp.cumsum(source_hot, axis=0) - source_hot
    slot_rank = jnp.sum(before * source_hot, axis=1)
    bucket = source * capacity + slot_rank
    request = (
        jnp.zeros((group_count * capacity,), jnp.int32)
        .at[bucket]
        .set(user_slot)
        .reshape(group_count, capacity)
    )
    requested = lax.all_to_all(request, "dp", split_axis=0, concat_axis=0, tiled=True)
    outgoing = jnp.take(item_emb, requested.reshape(-1), axis=0).reshape(
        group_count, capacity, model_width
    )
    arrived = lax.all_to_all(outgoing, "dp", split_axis=0, concat_axis=0, tiled=True)
    fetched = jnp.take(arrived.reshape(group_count * capacity, model_width), bucket, axis=0)
    embedded = jnp.where(alive_mask, fetched, jnp.zeros_like(fetched))

    def normalize(vector):
        return rms_scale(vector, user_gain)

    scaled, norm_back = jax.vjp(normalize, embedded.astype(jnp.float32))
    hidden = scaled.astype(jnp.bfloat16)
    key_rows = jnp.dot(hidden, weights, preferred_element_type=jnp.float32).astype(jnp.bfloat16)
    hidden_grad = lax.dot_general(
        key_grad, weights, (((1,), (1,)), ((), ())), preferred_element_type=jnp.float32
    )
    (embed_grad,) = norm_back(hidden_grad)
    pos_grad = jnp.where(alive_mask, embed_grad, jnp.zeros_like(embed_grad)).astype(jnp.bfloat16)
    weight_shard = lax.psum_scatter(
        lax.dot_general(
            hidden, key_grad, (((0,), (0,)), ((), ())), preferred_element_type=jnp.float32
        ),
        "fsdp",
        scatter_dimension=0,
        tiled=True,
    )
    weight_grad = lax.psum(weight_shard, "dp")
    scattered = (
        jnp.zeros((group_count * capacity, model_width), jnp.bfloat16)
        .at[bucket]
        .set(pos_grad)
        .reshape(group_count, capacity, model_width)
    )
    returned = lax.all_to_all(scattered, "dp", split_axis=0, concat_axis=0, tiled=True)
    item_table = (
        requested.reshape(1, group_count * capacity)
        == lax.broadcasted_iota(jnp.int32, (item_count, group_count * capacity), 0)
    ).astype(jnp.bfloat16)
    item_grad = jnp.dot(
        item_table,
        returned.reshape(group_count * capacity, model_width),
        preferred_element_type=jnp.float32,
    )
    (tokens_back,) = pool_back(item_grad)
    token_grads = tokens_back.reshape(item_count * block_rows, model_width).astype(jnp.bfloat16)
    return (key_rows, weight_grad, token_grads)


def solution(mesh):
    in_specs = (
        P(("dp", "fsdp"), None),
        P(("dp", "fsdp")),
        P(),
        P(("dp", "fsdp"), None),
        P(("dp", "fsdp")),
        P(("dp", "fsdp")),
        P(),
        P("fsdp", None),
        P(("dp", "fsdp"), None),
    )
    out_specs = (P(("dp", "fsdp"), None), P("fsdp", None), P(("dp", "fsdp"), None))
    return jax.shard_map(local, mesh=mesh, in_specs=in_specs, out_specs=out_specs, check_vma=False)
```

profile of v0, /device:TPU:6, one launch (start us, length us, event | category | flops | bytes accessed | tf_op | source)
XLA Modules:
  0.0 447.3 jit_solution(16365344587193851670)
XLA Ops:
  7.2 0.7 all-gather.2.cloned.1.call-update
  7.9 0.7 fusion.19
  8.6 0.6 reduce-window.6
  9.4 0.8 fusion.18
  10.2 0.7 and_reduce_fusion
  10.9 1.6 scatter_custom_fusion
  12.4 0.7 all_to_all.12
  13.1 11.2 %all-to-all-start = ((s32[16,1,24]{2,1,0:T(1,128)}), s32[16,1,24]{2,1,0:T(1,128)S(1)}, u32[]{:S(2)}, u32[]{:S(2)}) async-start(s32[16,1,24]{2,1,0:T(1,128)} %all_to_all.12), calls=%async_computation | async-start | bytes 16384 | tf_op jit(solution)/shard_map/all_to_all | solution.py:65
  24.4 0.8 convert_element_type.59
  25.2 1.0 fusion.27
  26.1 3.1 multiply_reduce_fusion.1
  29.2 2.1 multiply_reduce_fusion
  31.4 2.8 all-to-all-done
  34.3 0.5 broadcast.177
  34.8 0.7 reduce.13
  35.6 4.0 gather_fusion
  39.5 4.0 broadcast_select_fusion
  43.5 6.8 %all-to-all-start.1 = ((bf16[16,24,4096]{2,1,0:T(8,128)(2,1)}), bf16[16,24,4096]{2,1,0:T(8,128)(2,1)}, u32[]{:S(2)}, u32[]{:S(2)}) async-start(bf16[16,24,4096]{2,1,0:T(8,128)(2,1)} %broadcast_select_fusion), calls=%async_computation.1 | async-start | bytes 6291456 | tf_op jit(solution)/shard_map/all_to_all | solution.py:69
  51.2 71.9 %all-to-all-done.1 = bf16[16,24,4096]{2,1,0:T(8,128)(2,1)} async-done(((bf16[16,24,4096]{2,1,0:T(8,128)(2,1)}), bf16[16,24,4096]{2,1,0:T(8,128)(2,1)}, u32[]{:S(2)}, u32[]{:S(2)}) %all-to-all-start.1) | async-done | bytes 3145760 | tf_op jit(solution)/shard_map/all_to_all | solution.py:69
  123.1 6.2 %gather_fusion.1 = bf16[256,4096]{1,0:T(8,128)(2,1)S(1)} fusion(bf16[384,4096]{1,0:T(8,128)(2,1)} %bitcast.10, s32[1024]{0:T(1024)S(1)} %pad_clamp_fusion), kind=kCustom, calls=%fused_computation.1 | custom fusion | bytes 4195328 | tf_op jit(solution)/shard_map/jit(_take)/gather | solution.py:70
  129.4 8.3 %fusion.10 = (f32[256]{0:T(256)S(1)}, f32[256]{0:T(256)S(1)}, f32[256,4096]{1,0:T(8,128)}) fusion(bf16[256,4096]{1,0:T(8,128)(2,1)S(1)} %gather_fusion.1, pred[256]{0:T(512)(128)(4,1)S(1)} %get-tuple-element.5, pred[256]{0:T(512)(128)(4,1)S(1)} %iota_compare_fusion.5, f32[4096]{0:T(1024)S(1)} %copy-done.4, bf16[256,1024]{1,0:T(8,128)(2,1)S(1)} %copy-done, ...), kind=kOutput, calls=%fused_computation.25 | convolution fusion | flops 2155871744 | bytes 15223296 | tf_op jit(solution)/shard_map/dot_general | solution.py:79
  137.7 8.6 %fusion.13 = f32[4096,1024]{1,0:T(8,128)} fusion(bf16[256,1024]{1,0:T(8,128)(2,1)S(1)} %copy-done, f32[4096]{0:T(1024)S(1)} %copy-done.4, f32[256]{0:T(256)S(1)} %get-tuple-element.10, bf16[256,4096]{1,0:T(8,128)(2,1)S(1)} %gather_fusion.1, pred[256]{0:T(512)(128)(4,1)S(1)} %get-tuple-element.5, pred[256]{0:T(512)(128)(4,1)S(1)} %iota_compare_fusion.5), kind=kOutput, calls=%fused_computation.31 | convolution fusion | flops 2153775104 | bytes 19416576 | tf_op jit(solution)/shard_map/dot_general | solution.py:85
  146.3 8.3 %scatter_custom_fusion.1 = bf16[384,4096]{1,0:T(8,128)(2,1)} fusion(s32[256]{0:T(256)S(1)} %bitcast.64, bf16[]{:T(256)} %constant.57.clone.1, f32[256,4096]{1,0:T(8,128)} %get-tuple-element.13, f32[256]{0:T(256)S(1)} %get-tuple-element.9, f32[256]{0:T(256)S(1)} %get-tuple-element.10, pred[256]{0:T(512)(128)(4,1)S(1)} %iota_compare_fusion.5, ...), kind=kCustom, calls=%fused_computation.28 | custom fusion | flops 9437184 | bytes 9440258 | tf_op jit(solution)/shard_map/scatter | solution.py:96
  154.6 9.0 %all-to-all-start.2 = ((bf16[16,24,4096]{2,1,0:T(8,128)(2,1)}), bf16[16,24,4096]{2,1,0:T(8,128)(2,1)}, u32[]{:S(2)}, u32[]{:S(2)}) async-start(bf16[16,24,4096]{2,1,0:T(8,128)(2,1)} %bitcast.57), calls=%async_computation.3 | async-start | bytes 6291456 | tf_op jit(solution)/shard_map/all_to_all | solution.py:99
  163.7 108.4 %reduce-scatter.2.cloned.1.call-done = f32[256,1024]{1,0:T(8,128)} async-done(((f32[4096,1024]{1,0:T(8,128)}), f32[256,1024]{1,0:T(8,128)}) %reduce-scatter.2.cloned.1.call-update) | async-done | bytes 1048592 | tf_op jit(solution)/shard_map/reduce_scatter | solution.py:84
  272.2 6.6 %convolution_convert_fusion = bf16[256,1024]{1,0:T(8,128)(2,1)} fusion(bf16[4096,1024]{1,0:T(8,128)(2,1)} %all-gather.2.cloned.1.call-done, f32[4096]{0:T(1024)S(1)} %copy-done.4, f32[256]{0:T(256)S(1)} %get-tuple-element.10, bf16[256,4096]{1,0:T(8,128)(2,1)S(1)} %gather_fusion.1, pred[256]{0:T(512)(128)(4,1)S(1)} %get-tuple-element.5, ...), kind=kOutput, calls=%fused_computation.30 | convolution fusion | flops 2154037248 | bytes 11027968 | tf_op jit(solution)/shard_map/dot_general | solution.py:78
  278.8 1.4 all-to-all-done.2
  280.1 2.6 convolution_divide_fusion
  282.7 3.7 fusion.4
  286.4 4.3 fusion
  290.7 147.7 %all-reduce.2.cloned.1.call-done = f32[256,1024]{1,0:T(8,128)} async-done(((f32[256,1024]{1,0:T(8,128)}), f32[256,1024]{1,0:T(8,128)}) %all-reduce.2.cloned.1.call-update) | async-done | bytes 1048592 | tf_op jit(solution)/shard_map/psum | solution.py:92
  438.4 2.3 copy.18
  (30 shorter events, 0.9 us)
Async XLA Ops:
  7.2 122.2 %copy-start = (bf16[256,1024]{1,0:T(8,128)(2,1)S(1)}, bf16[256,1024]{1,0:T(8,128)(2,1)}, u32[]{:S(2)}) copy-start(bf16[256,1024]{1,0:T(8,128)(2,1)} %param.17) | copy-start | bytes 1572868
  7.2 22.0 %copy-start.3 = (f32[4096]{0:T(1024)S(1)}, f32[4096]{0:T(1024)}, u32[]{:S(2)}) copy-start(f32[4096]{0:T(1024)} %param.11) | copy-start | bytes 49156
  7.2 122.2 %all-gather.2.cloned.1.call-start = ((), (), s32[]{:S(2)}) async-start(), calls=%async_computation.4 | async-start | bytes 8912896 | tf_op jit(solution)/shard_map/all_gather | solution.py:44
  13.1 21.1 %all-to-all-start = ((s32[16,1,24]{2,1,0:T(1,128)}), s32[16,1,24]{2,1,0:T(1,128)S(1)}, u32[]{:S(2)}, u32[]{:S(2)}) async-start(s32[16,1,24]{2,1,0:T(1,128)} %all_to_all.12), calls=%async_computation | async-start | bytes 16384 | tf_op jit(solution)/shard_map/all_to_all | solution.py:65
  24.4 4.9 %copy-start.1 = (bf16[512,4096]{1,0:T(8,128)(2,1)S(1)}, bf16[512,4096]{1,0:T(8,128)(2,1)}, u32[]{:S(2)}) copy-start(bf16[512,4096]{1,0:T(8,128)(2,1)} %param.9) | copy-start | bytes 12582916
  43.5 79.6 %all-to-all-start.1 = ((bf16[16,24,4096]{2,1,0:T(8,128)(2,1)}), bf16[16,24,4096]{2,1,0:T(8,128)(2,1)}, u32[]{:S(2)}, u32[]{:S(2)}) async-start(bf16[16,24,4096]{2,1,0:T(8,128)(2,1)} %broadcast_select_fusion), calls=%async_computation.1 | async-start | bytes 6291456 | tf_op jit(solution)/shard_map/all_to_all | solution.py:69
  50.3 221.8 %reduce-scatter.2.cloned.1.call-start = ((), (), s32[]{:S(2)}) async-start(), calls=%async_computation.5 | async-start | bytes 17825792 | tf_op jit(solution)/shard_map/reduce_scatter | solution.py:84
  123.1 6.2 %copy-start.4 = (f32[4096]{0:T(1024)S(1)}, f32[4096]{0:T(1024)}, u32[]{:S(2)}) copy-start(f32[4096]{0:T(1024)} %param.15) | copy-start | bytes 49156
  154.6 125.5 %all-to-all-start.2 = ((bf16[16,24,4096]{2,1,0:T(8,128)(2,1)}), bf16[16,24,4096]{2,1,0:T(8,128)(2,1)}, u32[]{:S(2)}, u32[]{:S(2)}) async-start(bf16[16,24,4096]{2,1,0:T(8,128)(2,1)} %bitcast.57), calls=%async_computation.3 | async-start | bytes 6291456 | tf_op jit(solution)/shard_map/all_to_all | solution.py:99
  163.6 274.8 %all-reduce.2.cloned.1.call-start = ((), (), s32[]{:S(2)}) async-start(), calls=%async_computation.6 | async-start | bytes 2097152 | tf_op jit(solution)/shard_map/psum | solution.py:92
  280.1 6.3 %copy-start.2 = (bf16[512,4096]{1,0:T(8,128)(2,1)S(1)}, bf16[512,4096]{1,0:T(8,128)(2,1)}, u32[]{:S(2)}) copy-start(bf16[512,4096]{1,0:T(8,128)(2,1)} %param.9) | copy-start | bytes 12582916
Sparse Core Ops, SparseCore 0:
  9.9 73.4 all-gather.1
  146.4 125.6 reduce-scatter.1
  274.8 163.6 all-reduce.1
where the time goes:
time: 448 us; the launch traced here: 447 us
  waiting for transfers between devices  333 us (74%)
  other arithmetic  30.8 us (7%)
  starting transfers between devices  27.3 us (6%)
  matrix products  26 us (6%)
  local copies, waits for them, and re-layouts  15.6 us (3%)
  between operations  14.6 us (3%)
    psum x1, waiting for transfers between devices, local(): weight_grad = lax.psum(weight_shard, 'dp')  148 us
    reduce_scatter x1, waiting for transfers between devices, local(): lax.psum_scatter(lax.dot_general(hidden, key_grad, (((0,), (0,)), ((), ()...  108 us
    all_to_all x1, waiting for transfers between devices, local(): lax.all_to_all(outgoing, 'dp', split_axis=0, concat_axis=0, tiled=True)  71.9 us
    all_to_all x1, starting transfers between devices, local(): lax.all_to_all(request, 'dp', split_axis=0, concat_axis=0, tiled=True)  11.2 us
    all_to_all x1, starting transfers between devices, local(): lax.all_to_all(scattered, 'dp', split_axis=0, concat_axis=0, tiled=True)  8.99 us
  transfers between devices with their start and end apart: 6, of which 5 were waited for; matrix products, arithmetic and copies ran while one was open for 12% of the time, Pallas kernels for 0%

commit v1 on v0

--- a/solution.py
+++ b/solution.py
@@ -42,6 +42,7 @@
     pooled, pool_back = jax.vjp(pooling, stacked_tokens.astype(jnp.float32))
     item_emb = pooled.astype(jnp.bfloat16)
     weights = lax.all_gather(key_weight, "fsdp", axis=0, tiled=True)
+    grads_all = lax.all_gather(key_grad, "fsdp", axis=0, tiled=True)
     row_count = user_slot.shape[0]
     source = user_source[:, 0]
     seq_count = user_lengths.shape[0]
@@ -49,26 +50,19 @@
     alive_mask = (
         lax.broadcasted_iota(jnp.int32, (seq_count, seq_rows), 1) < user_lengths[:, None]
     ).reshape(row_count, 1)
-    capacity = 3 * row_count // (2 * group_count)
-    source_hot = (
-        source[:, None] == lax.broadcasted_iota(jnp.int32, (row_count, group_count), 1)
-    ).astype(jnp.int32)
-    before = jnp.cumsum(source_hot, axis=0) - source_hot
-    slot_rank = jnp.sum(before * source_hot, axis=1)
-    bucket = source * capacity + slot_rank
-    request = (
-        jnp.zeros((group_count * capacity,), jnp.int32)
-        .at[bucket]
-        .set(user_slot)
-        .reshape(group_count, capacity)
-    )
-    requested = lax.all_to_all(request, "dp", split_axis=0, concat_axis=0, tiled=True)
-    outgoing = jnp.take(item_emb, requested.reshape(-1), axis=0).reshape(
-        group_count, capacity, model_width
-    )
-    arrived = lax.all_to_all(outgoing, "dp", split_axis=0, concat_axis=0, tiled=True)
-    fetched = jnp.take(arrived.reshape(group_count * capacity, model_width), bucket, axis=0)
-    embedded = jnp.where(alive_mask, fetched, jnp.zeros_like(fetched))
+    table = lax.all_to_all(
+        jnp.broadcast_to(item_emb[None], (group_count, item_count, model_width)),
+        "dp",
+        split_axis=0,
+        concat_axis=0,
+        tiled=True,
+    ).reshape(group_count * item_count, model_width)
+    item_index = source * item_count + user_slot
+    pick = (
+        (item_index[:, None] == lax.broadcasted_iota(jnp.int32, (row_count, group_count * item_count), 1))
+        & alive_mask
+    ).astype(jnp.bfloat16)
+    embedded = jnp.dot(pick, table, preferred_element_type=jnp.float32).astype(jnp.bfloat16)
 
     def normalize(vector):
         return rms_scale(vector, user_gain)
@@ -81,30 +75,29 @@
     )
     (embed_grad,) = norm_back(hidden_grad)
     pos_grad = jnp.where(alive_mask, embed_grad, jnp.zeros_like(embed_grad)).astype(jnp.bfloat16)
-    weight_shard = lax.psum_scatter(
-        lax.dot_general(
-            hidden, key_grad, (((0,), (0,)), ((), ())), preferred_element_type=jnp.float32
+    hidden_cols = lax.all_to_all(hidden, "fsdp", split_axis=1, concat_axis=0, tiled=True)
+    weight_part = lax.dot_general(
+        hidden_cols, grads_all, (((0,), (0,)), ((), ())), preferred_element_type=jnp.float32
+    )
+    weight_rows = weight_part.shape[0]
+    reduced = jnp.sum(
+        lax.all_to_all(weight_part, "dp", split_axis=0, concat_axis=0, tiled=True).reshape(
+            group_count, weight_rows // group_count, weight_part.shape[1]
         ),
-        "fsdp",
-        scatter_dimension=0,
+        axis=0,
+    )
+    weight_grad = lax.all_to_all(
+        jnp.broadcast_to(reduced[None], (group_count,) + reduced.shape),
+        "dp",
+        split_axis=0,
+        concat_axis=0,
         tiled=True,
-    )
-    weight_grad = lax.psum(weight_shard, "dp")
-    scattered = (
-        jnp.zeros((group_count * capacity, model_width), jnp.bfloat16)
-        .at[bucket]
-        .set(pos_grad)
-        .reshape(group_count, capacity, model_width)
-    )
-    returned = lax.all_to_all(scattered, "dp", split_axis=0, concat_axis=0, tiled=True)
-    item_table = (
-        requested.reshape(1, group_count * capacity)
-        == lax.broadcasted_iota(jnp.int32, (item_count, group_count * capacity), 0)
-    ).astype(jnp.bfloat16)
-    item_grad = jnp.dot(
-        item_table,
-        returned.reshape(group_count * capacity, model_width),
-        preferred_element_type=jnp.float32,
+    ).reshape(weight_rows, weight_part.shape[1])
+    item_part = lax.dot_general(
+        pick, pos_grad, (((0,), (0,)), ((), ())), preferred_element_type=jnp.float32
+    ).reshape(group_count, item_count, model_width)
+    item_grad = jnp.sum(
+        lax.all_to_all(item_part, "dp", split_axis=0, concat_axis=0, tiled=True), axis=0
     )
     (tokens_back,) = pool_back(item_grad)
     token_grads = tokens_back.reshape(item_count * block_rows, model_width).astype(jnp.bfloat16)

time: 448 us -> 275 us (0.61)
  waiting for transfers between devices: 333 us -> 127 us
  blocking collectives: 0 us -> 48.6 us
  other arithmetic: 30.8 us -> 18.7 us
  local copies, waits for them, and re-layouts: 15.6 us -> 9.04 us
    psum x1 -> x0, waiting for transfers between devices: 148 us -> none  [local(): weight_grad = lax.psum(weight_shard, 'dp')]
    reduce_scatter x1 -> x0, waiting for transfers between devices: 108 us -> none  [local(): lax.psum_scatter(lax.dot_general(hidden, key_grad, (((0,), (0,)), ((), ()...]
    all_to_all x0 -> x1, blocking collectives: none -> 48.6 us  [local(): lax.all_to_all(hidden, 'fsdp', split_axis=1, concat_axis=0, tiled=True)]
    all_gather x1, waiting for transfers between devices: 0.02 us -> 26.9 us  [local(): weights = lax.all_gather(key_weight, 'fsdp', axis=0, tiled=True)]
    all_gather x0 -> x1, waiting for transfers between devices: none -> 17.7 us  [local(): grads_all = lax.all_gather(key_grad, 'fsdp', axis=0, tiled=True)]
    gather x2 -> x0, local copies, waits for them, and re-layouts: 10.2 us -> none  [the longest x1 6.19 us: local(): jnp.take(arrived.reshape(group_count * capacity, model_width), bucket, ax...]
    scatter x1 -> x0, other arithmetic: 8.34 us -> none  [local(): scattered = jnp.zeros((group_count * capacity, model_width), jnp.bfloat16...]
    all_to_all x3 -> x4, waiting for transfers between devices: 76.1 us -> 81.2 us  [the longest x1 27.5 us: local(): lax.all_to_all(item_part, 'dp', split_axis=0, concat_axis=0, tiled=True)]
  transfers between devices with their start and end apart: 6 -> 6, of which waited for: 5 -> 6; matrix products, arithmetic and copies ran while one was open for 12% -> 16% of each run, Pallas kernels for 0% -> 0%
where the time goes in v1:
time: 275 us; the launch traced here: 274 us
  waiting for transfers between devices  127 us (46%)
  blocking collectives  48.6 us (18%)
  starting transfers between devices  29.5 us (11%)
  matrix products  25.8 us (9%)
  other arithmetic  18.7 us (7%)
  between operations  14.9 us (5%)
  local copies, waits for them, and re-layouts  9.04 us (3%)
    all_to_all x1, blocking collectives, local(): lax.all_to_all(hidden, 'fsdp', split_axis=1, concat_axis=0, tiled=True)  48.6 us
    all_to_all x1, waiting for transfers between devices, local(): lax.all_to_all(item_part, 'dp', split_axis=0, concat_axis=0, tiled=True)  27.5 us
    all_gather x1, waiting for transfers between devices, local(): weights = lax.all_gather(key_weight, 'fsdp', axis=0, tiled=True)  26.9 us
    all_to_all x1, waiting for transfers between devices, local(): lax.all_to_all(weight_part, 'dp', split_axis=0, concat_axis=0, tiled=True)  24.5 us
    all_gather x1, waiting for transfers between devices, local(): grads_all = lax.all_gather(key_grad, 'fsdp', axis=0, tiled=True)  17.7 us
    all_to_all x1, waiting for transfers between devices, local(): lax.all_to_all(jnp.broadcast_to(item_emb[None], (group_count, item_count,...  16.5 us
    all_to_all x1, waiting for transfers between devices, local(): lax.all_to_all(jnp.broadcast_to(reduced[None], (group_count,) + reduced.s...  12.6 us
    all_to_all x1, starting transfers between devices, local(): lax.all_to_all(jnp.broadcast_to(item_emb[None], (group_count, item_count,...  11.2 us
  transfers between devices with their start and end apart: 6, of which 6 were waited for; matrix products, arithmetic and copies ran while one was open for 16% of the time, Pallas kernels for 0%

profile of v1, /device:TPU:6, one launch (start us, length us, event | category | flops | bytes accessed | tf_op | source)
XLA Modules:
  0.0 273.7 jit_solution(17595173814519701098)
XLA Ops:
  7.2 0.7 all-gather.3.cloned.1.call-update
  8.0 0.7 all-gather.5.cloned.1.call-update
  8.7 0.8 convert_element_type.57
  9.5 0.9 fusion.25
  10.4 3.1 %multiply_reduce_fusion.1 = f32[512]{0:T(512)S(1)} fusion(bf16[512,4096]{1,0:T(8,128)(2,1)} %param.9), kind=kLoop, calls=%fused_computation.10 | loop fusion | flops 6290944 | bytes 4196352 | tf_op jit(solution)/shard_map/jvp()/reduce_sum | solution.py:10
  13.5 2.1 multiply_reduce_fusion
  15.7 1.0 broadcast_in_dim.22
  16.7 11.2 %all-to-all-start = ((bf16[16,4,4096]{2,1,0:T(4,128)(2,1)}), bf16[16,4,4096]{2,1,0:T(4,128)(2,1)S(1)}, u32[]{:S(2)}, u32[]{:S(2)}) async-start(bf16[16,4,4096]{2,1,0:T(4,128)(2,1)} %broadcast_in_dim.22), calls=%async_computation | async-start | bytes 1048576 | tf_op jit(solution)/shard_map/all_to_all | solution.py:53
  28.7 16.5 %all-to-all-done = bf16[16,4,4096]{2,1,0:T(4,128)(2,1)S(1)} async-done(((bf16[16,4,4096]{2,1,0:T(4,128)(2,1)}), bf16[16,4,4096]{2,1,0:T(4,128)(2,1)S(1)}, u32[]{:S(2)}, u32[]{:S(2)}) %all-to-all-start) | async-done | bytes 524320 | tf_op jit(solution)/shard_map/all_to_all | solution.py:53
  45.3 0.8 convolution_convert_fusion
  46.0 26.9 %all-gather.3.cloned.1.call-done = bf16[4096,1024]{1,0:T(8,128)(2,1)} async-done(((bf16[256,1024]{1,0:T(8,128)(2,1)}), bf16[4096,1024]{1,0:T(8,128)(2,1)}) %all-gather.3.cloned.1.call-update) | async-done | bytes 8388624 | tf_op jit(solution)/shard_map/all_gather | solution.py:44
  72.9 8.0 %fusion.12 = (f32[256]{0:T(256)S(1)}, f32[256]{0:T(256)S(1)}, f32[256,4096]{1,0:T(8,128)}) fusion(bf16[256,4096]{1,0:T(8,128)(2,1)S(1)} %convolution_convert_fusion, f32[4096]{0:T(1024)S(1)} %copy-done.7, bf16[256,1024]{1,0:T(8,128)(2,1)S(1)} %copy-done.5, bf16[4096,1024]{1,0:T(8,128)(2,1)} %all-gather.3.cloned.1.call-done), kind=kOutput, calls=%fused_computation.23 | convolution fusion | flops 2153774592 | bytes 15222784 | tf_op jit(solution)/shard_map/dot_general | solution.py:73
  80.9 0.7 fusion.11
  81.9 48.6 %all_to_all.40 = bf16[256,16,256]{2,0,1:T(8,128)(2,1)} all-to-all(bf16[256,16,256]{2,0,1:T(8,128)(2,1)S(1)} %bitcast.43), channel_id=1, replica_groups=mesh['dp'=16,'fsdp'=16] {'fsdp'}, dimensions={1} | all-to-all | bytes 4194304 | tf_op jit(solution)/shard_map/all_to_all | solution.py:78
  130.4 4.1 %copy.13 = bf16[256,4096]{1,0:T(8,128)(2,1)} copy(bf16[256,4096]{0,1:T(8,128)(2,1)} %bitcast.42) | data formatting | bytes 4194304 | tf_op jit(solution)/shard_map/dot_general | solution.py:79
  134.5 17.7 %all-gather.5.cloned.1.call-done = bf16[4096,1024]{1,0:T(8,128)(2,1)} async-done(((bf16[256,1024]{1,0:T(8,128)(2,1)}), bf16[4096,1024]{1,0:T(8,128)(2,1)}) %all-gather.5.cloned.1.call-update) | async-done | bytes 8388624 | tf_op jit(solution)/shard_map/all_gather | solution.py:45
  152.3 7.3 %fusion.5 = f32[16,16,1024]{2,1,0:T(8,128)} fusion(bf16[16,16,4096]{2,1,0:T(8,128)(2,1)} %bitcast.45, bf16[4096,1024]{1,0:T(8,128)(2,1)} %all-gather.5.cloned.1.call-done), kind=kOutput, calls=%fused_computation.7 | convolution fusion | flops 2147483648 | bytes 11534336 | tf_op jit(solution)/shard_map/dot_general | solution.py:79
  159.6 9.5 %all-to-all-start.2 = ((f32[16,16,1024]{2,1,0:T(8,128)}), f32[16,16,1024]{2,1,0:T(8,128)}, u32[]{:S(2)}, u32[]{:S(2)}) async-start(f32[16,16,1024]{2,1,0:T(8,128)} %fusion.5), calls=%async_computation.2 | async-start | bytes 2097152 | tf_op jit(solution)/shard_map/all_to_all | solution.py:84
  169.1 3.3 %fusion.13 = f32[64,4096]{1,0:T(8,128)S(1)} fusion(bf16[256,4096]{1,0:T(8,128)(2,1)S(1)} %convolution_convert_fusion, f32[256,4096]{1,0:T(8,128)} %get-tuple-element.11, f32[256]{0:T(256)S(1)} %get-tuple-element.7, f32[256]{0:T(256)S(1)} %get-tuple-element.8, pred[256]{0:T(512)(128)(4,1)S(1)} %iota_compare_fusion.2, s32[256]{0:T(256)S(1)} %add.32), kind=kOutput, calls=%fused_computation.25 | convolution fusion | flops 141590528 | bytes 7343360 | tf_op jit(solution)/shard_map/dot_general | solution.py:96
  172.4 1.3 reshape.136
  173.7 24.5 %all-to-all-done.2 = f32[16,16,1024]{2,1,0:T(8,128)} async-done(((f32[16,16,1024]{2,1,0:T(8,128)}), f32[16,16,1024]{2,1,0:T(8,128)}, u32[]{:S(2)}, u32[]{:S(2)}) %all-to-all-start.2) | async-done | bytes 1048608 | tf_op jit(solution)/shard_map/all_to_all | solution.py:84
  198.2 4.4 %all-to-all-start.4 = ((f32[16,4,4096]{2,1,0:T(4,128)}), f32[16,4,4096]{2,1,0:T(4,128)S(1)}, u32[]{:S(2)}, u32[]{:S(2)}) async-start(f32[16,4,4096]{2,1,0:T(4,128)} %reshape.136), calls=%async_computation.4 | async-start | bytes 2097152 | tf_op jit(solution)/shard_map/all_to_all | solution.py:100
  202.6 1.3 reduce_sum.74
  203.8 27.5 %all-to-all-done.4 = f32[16,4,4096]{2,1,0:T(4,128)S(1)} async-done(((f32[16,4,4096]{2,1,0:T(4,128)}), f32[16,4,4096]{2,1,0:T(4,128)S(1)}, u32[]{:S(2)}, u32[]{:S(2)}) %all-to-all-start.4) | async-done | bytes 1048608 | tf_op jit(solution)/shard_map/all_to_all | solution.py:100
  231.4 1.2 broadcast_in_dim.23
  232.7 4.4 %all-to-all-start.3 = ((f32[16,16,1024]{2,1,0:T(8,128)}), f32[16,16,1024]{2,1,0:T(8,128)S(1)}, u32[]{:S(2)}, u32[]{:S(2)}) async-start(f32[16,16,1024]{2,1,0:T(8,128)} %broadcast_in_dim.23), calls=%async_computation.3 | async-start | bytes 2097152 | tf_op jit(solution)/shard_map/all_to_all | solution.py:89
  237.1 6.5 %convolution_convert_fusion.1 = bf16[256,1024]{1,0:T(8,128)(2,1)} fusion(bf16[256,4096]{1,0:T(8,128)(2,1)S(1)} %copy-done.3, bf16[4096,1024]{1,0:T(8,128)(2,1)} %all-gather.3.cloned.1.call-done), kind=kOutput, calls=%fused_computation.26 | convolution fusion | flops 2147745792 | bytes 11010048 | tf_op jit(solution)/shard_map/dot_general | solution.py:72
  243.6 1.4 reduce_sum.76
  245.1 3.9 %fusion.4 = f32[512]{0:T(512)S(1)} fusion(bf16[512,4096]{1,0:T(8,128)(2,1)} %param.9, f32[4096]{0:T(1024)S(1)} %copy-done.6, f32[512]{0:T(512)S(1)} %get-tuple-element.9, f32[4,4096]{1,0:T(4,128)S(1)} %broadcast_divide_fusion), kind=kLoop, calls=%fused_computation.6 | loop fusion | flops 10485248 | bytes 4280320 | tf_op jit(solution)/shard_map/transpose(jvp())/reduce_sum | solution.py:10
  248.9 4.3 %fusion = bf16[512,4096]{1,0:T(8,128)(2,1)} fusion(bf16[512,4096]{1,0:T(8,128)(2,1)S(1)} %copy-done.1, f32[512]{0:T(512)S(1)} %multiply_multiply_fusion, f32[512]{0:T(512)S(1)} %get-tuple-element.5, f32[4096]{0:T(1024)S(1)} %copy-done.6, f32[512]{0:T(512)S(1)} %get-tuple-element.9, f32[4,4096]{1,0:T(4,128)S(1)} %broadcast_divide_fusion), kind=kLoop, calls=%fused_computation.1 | loop fusion | flops 16777216 | bytes 8476672 | tf_op jit(solution)/shard_map/convert_element_type | solution.py:103
  253.2 12.6 %all-to-all-done.3 = f32[16,16,1024]{2,1,0:T(8,128)S(1)} async-done(((f32[16,16,1024]{2,1,0:T(8,128)}), f32[16,16,1024]{2,1,0:T(8,128)S(1)}, u32[]{:S(2)}, u32[]{:S(2)}) %all-to-all-start.3) | async-done | bytes 1048608 | tf_op jit(solution)/shard_map/all_to_all | solution.py:89
  265.9 1.0 copy.19
  (32 shorter events, 0.7 us)
Async XLA Ops:
  7.2 6.3 %copy-start.6 = (f32[4096]{0:T(1024)S(1)}, f32[4096]{0:T(1024)}, u32[]{:S(2)}) copy-start(f32[4096]{0:T(1024)} %param.11) | copy-start | bytes 49156
  7.2 65.7 %all-gather.3.cloned.1.call-start = ((), (), s32[]{:S(2)}) async-start(), calls=%async_computation.5 | async-start | bytes 8912896 | tf_op jit(solution)/shard_map/all_gather | solution.py:44
  7.9 144.4 %all-gather.5.cloned.1.call-start = ((), (), s32[]{:S(2)}) async-start(), calls=%async_computation.6 | async-start | bytes 8912896 | tf_op jit(solution)/shard_map/all_gather | solution.py:45
  8.7 4.9 %copy-start = (bf16[512,4096]{1,0:T(8,128)(2,1)S(1)}, bf16[512,4096]{1,0:T(8,128)(2,1)}, u32[]{:S(2)}) copy-start(bf16[512,4096]{1,0:T(8,128)(2,1)} %param.9) | copy-start | bytes 12582916
  10.4 18.2 %copy-start.9 = (s32[256,1]{0,1:T(1,128)S(1)}, s32[256,1]{0,1:T(1,128)}, u32[]{:S(2)}) copy-start(s32[256,1]{0,1:T(1,128)} %param.12) | copy-start | bytes 3076
  10.4 18.2 %copy-start.8 = (s32[256]{0:T(256)S(1)}, s32[256]{0:T(256)}, u32[]{:S(2)}) copy-start(s32[256]{0:T(256)} %param.13) | copy-start | bytes 3076
  13.5 59.4 %copy-start.5 = (bf16[256,1024]{1,0:T(8,128)(2,1)S(1)}, bf16[256,1024]{1,0:T(8,128)(2,1)}, u32[]{:S(2)}) copy-start(bf16[256,1024]{1,0:T(8,128)(2,1)} %param.17) | copy-start | bytes 1572868
  13.5 59.4 %copy-start.7 = (f32[4096]{0:T(1024)S(1)}, f32[4096]{0:T(1024)}, u32[]{:S(2)}) copy-start(f32[4096]{0:T(1024)} %param.15) | copy-start | bytes 49156
  16.7 28.4 %all-to-all-start = ((bf16[16,4,4096]{2,1,0:T(4,128)(2,1)}), bf16[16,4,4096]{2,1,0:T(4,128)(2,1)S(1)}, u32[]{:S(2)}, u32[]{:S(2)}) async-start(bf16[16,4,4096]{2,1,0:T(4,128)(2,1)} %broadcast_in_dim.22), calls=%async_computation | async-start | bytes 1048576 | tf_op jit(solution)/shard_map/all_to_all | solution.py:53
  81.6 48.8 %copy-start.2 = (bf16[256,4096]{1,0:T(8,128)(2,1)}, bf16[256,4096]{1,0:T(8,128)(2,1)S(1)}, u32[]{:S(2)}) copy-start(bf16[256,4096]{1,0:T(8,128)(2,1)S(1)} %fusion.11) | copy-start | bytes 6291460
  159.6 38.6 %all-to-all-start.2 = ((f32[16,16,1024]{2,1,0:T(8,128)}), f32[16,16,1024]{2,1,0:T(8,128)}, u32[]{:S(2)}, u32[]{:S(2)}) async-start(f32[16,16,1024]{2,1,0:T(8,128)} %fusion.5), calls=%async_computation.2 | async-start | bytes 2097152 | tf_op jit(solution)/shard_map/all_to_all | solution.py:84
  172.4 64.7 %copy-start.3 = (bf16[256,4096]{1,0:T(8,128)(2,1)S(1)}, bf16[256,4096]{1,0:T(8,128)(2,1)}, u32[]{:S(2)}) copy-start(bf16[256,4096]{1,0:T(8,128)(2,1)} %copy-done.2) | copy-start | bytes 6291460
  198.2 33.2 %all-to-all-start.4 = ((f32[16,4,4096]{2,1,0:T(4,128)}), f32[16,4,4096]{2,1,0:T(4,128)S(1)}, u32[]{:S(2)}, u32[]{:S(2)}) async-start(f32[16,4,4096]{2,1,0:T(4,128)} %reshape.136), calls=%async_computation.4 | async-start | bytes 2097152 | tf_op jit(solution)/shard_map/all_to_all | solution.py:100
  231.4 1.3 copy-start.4
  232.7 33.2 %all-to-all-start.3 = ((f32[16,16,1024]{2,1,0:T(8,128)}), f32[16,16,1024]{2,1,0:T(8,128)S(1)}, u32[]{:S(2)}, u32[]{:S(2)}) async-start(f32[16,16,1024]{2,1,0:T(8,128)} %broadcast_in_dim.23), calls=%async_computation.3 | async-start | bytes 2097152 | tf_op jit(solution)/shard_map/all_to_all | solution.py:89
  245.0 4.0 %copy-start.1 = (bf16[512,4096]{1,0:T(8,128)(2,1)S(1)}, bf16[512,4096]{1,0:T(8,128)(2,1)}, u32[]{:S(2)}) copy-start(bf16[512,4096]{1,0:T(8,128)(2,1)} %param.9) | copy-start | bytes 12582916
Sparse Core Ops, SparseCore 0:
  9.8 63.0 all-gather.2
  74.7 77.4 all-gather.4

commit v2 on v1

--- a/solution.py
+++ b/solution.py
@@ -42,7 +42,12 @@
     pooled, pool_back = jax.vjp(pooling, stacked_tokens.astype(jnp.float32))
     item_emb = pooled.astype(jnp.bfloat16)
     weights = lax.all_gather(key_weight, "fsdp", axis=0, tiled=True)
-    grads_all = lax.all_gather(key_grad, "fsdp", axis=0, tiled=True)
+    part_count = 2
+    part_width = key_grad.shape[1] // part_count
+    grad_parts = [
+        lax.all_gather(key_grad[:, k * part_width : (k + 1) * part_width], "fsdp", axis=0, tiled=True)
+        for k in range(part_count)
+    ]
     row_count = user_slot.shape[0]
     source = user_source[:, 0]
     seq_count = user_lengths.shape[0]
@@ -75,30 +80,40 @@
     )
     (embed_grad,) = norm_back(hidden_grad)
     pos_grad = jnp.where(alive_mask, embed_grad, jnp.zeros_like(embed_grad)).astype(jnp.bfloat16)
-    hidden_cols = lax.all_to_all(hidden, "fsdp", split_axis=1, concat_axis=0, tiled=True)
-    weight_part = lax.dot_general(
-        hidden_cols, grads_all, (((0,), (0,)), ((), ())), preferred_element_type=jnp.float32
-    )
-    weight_rows = weight_part.shape[0]
-    reduced = jnp.sum(
-        lax.all_to_all(weight_part, "dp", split_axis=0, concat_axis=0, tiled=True).reshape(
-            group_count, weight_rows // group_count, weight_part.shape[1]
-        ),
-        axis=0,
-    )
-    weight_grad = lax.all_to_all(
-        jnp.broadcast_to(reduced[None], (group_count,) + reduced.shape),
-        "dp",
-        split_axis=0,
-        concat_axis=0,
-        tiled=True,
-    ).reshape(weight_rows, weight_part.shape[1])
     item_part = lax.dot_general(
         pick, pos_grad, (((0,), (0,)), ((), ())), preferred_element_type=jnp.float32
     ).reshape(group_count, item_count, model_width)
     item_grad = jnp.sum(
         lax.all_to_all(item_part, "dp", split_axis=0, concat_axis=0, tiled=True), axis=0
     )
+    item_grad, grad_parts[0] = lax.optimization_barrier((item_grad, grad_parts[0]))
+    fsdp_count = lax.axis_size("fsdp")
+    hidden_split = hidden.reshape(row_count, fsdp_count, model_width // fsdp_count).transpose(1, 0, 2)
+    hidden_cols = lax.all_to_all(hidden_split, "fsdp", split_axis=0, concat_axis=0, tiled=True).reshape(
+        fsdp_count * row_count, model_width // fsdp_count
+    )
+    weight_rows = hidden_cols.shape[1]
+    pieces = []
+    for grads_all in grad_parts:
+        weight_part = lax.dot_general(
+            hidden_cols, grads_all, (((0,), (0,)), ((), ())), preferred_element_type=jnp.float32
+        )
+        reduced = jnp.sum(
+            lax.all_to_all(weight_part, "dp", split_axis=0, concat_axis=0, tiled=True).reshape(
+                group_count, weight_rows // group_count, part_width
+            ),
+            axis=0,
+        )
+        pieces.append(
+            lax.all_to_all(
+                jnp.broadcast_to(reduced[None], (group_count,) + reduced.shape),
+                "dp",
+                split_axis=0,
+                concat_axis=0,
+                tiled=True,
+            ).reshape(weight_rows, part_width)
+        )
+    weight_grad = jnp.concatenate(pieces, axis=1)
     (tokens_back,) = pool_back(item_grad)
     token_grads = tokens_back.reshape(item_count * block_rows, model_width).astype(jnp.bfloat16)
     return (key_rows, weight_grad, token_grads)

time: 275 us -> 271 us (0.985)
  blocking collectives: 48.6 us -> 0 us
  starting transfers between devices: 29.5 us -> 51.3 us
  waiting for transfers between devices: 127 us -> 146 us
  local copies, waits for them, and re-layouts: 9.04 us -> 11.8 us
    all_to_all x1 -> x0, blocking collectives: 48.6 us -> none  [local(): lax.all_to_all(hidden, 'fsdp', split_axis=1, concat_axis=0, tiled=True)]
    all_to_all x0 -> x1, waiting for transfers between devices: none -> 33.4 us  [local(): lax.all_to_all(hidden_split, 'fsdp', split_axis=0, concat_axis=0, tiled=T...]
    all_to_all x1 -> x2, waiting for transfers between devices: 24.5 us -> 17.3 us  [local(): lax.all_to_all(weight_part, 'dp', split_axis=0, concat_axis=0, tiled=True)]
    all_to_all x1, waiting for transfers between devices: 27.5 us -> 20.8 us  [local(): lax.all_to_all(item_part, 'dp', split_axis=0, concat_axis=0, tiled=True)]
    all_to_all x1 -> x2, starting transfers between devices: 9.53 us -> 15.9 us  [local(): lax.all_to_all(weight_part, 'dp', split_axis=0, concat_axis=0, tiled=True)]
    all_to_all x1 -> x2, waiting for transfers between devices: 12.6 us -> 18.9 us  [local(): lax.all_to_all(jnp.broadcast_to(reduced[None], (group_count,) + reduced.s...]
    all_to_all x1, starting transfers between devices: 4.35 us -> 9.67 us  [local(): lax.all_to_all(item_part, 'dp', split_axis=0, concat_axis=0, tiled=True)]
    all_gather x1 -> x2, waiting for transfers between devices: 17.7 us -> 12.5 us  [local(): lax.all_gather(key_grad[:, k * part_width:(k + 1) * part_width], 'fsdp',...]
  transfers between devices with their start and end apart: 6 -> 10, of which waited for: 6 -> 8; matrix products, arithmetic and copies ran while one was open for 16% -> 20% of each run, Pallas kernels for 0% -> 0%
where the time goes in v2:
time: 271 us; the launch traced here: 269 us
  waiting for transfers between devices  146 us (54%)
  starting transfers between devices  51.3 us (19%)
  matrix products  28.4 us (10%)
  other arithmetic  17.3 us (6%)
  between operations  14.7 us (5%)
  local copies, waits for them, and re-layouts  11.8 us (4%)
    all_to_all x1, waiting for transfers between devices, local(): lax.all_to_all(hidden_split, 'fsdp', split_axis=0, concat_axis=0, tiled=T...  33.4 us
    all_gather x1, waiting for transfers between devices, local(): weights = lax.all_gather(key_weight, 'fsdp', axis=0, tiled=True)  24.9 us
    all_to_all x1, waiting for transfers between devices, local(): lax.all_to_all(item_part, 'dp', split_axis=0, concat_axis=0, tiled=True)  20.8 us
    all_to_all x2, waiting for transfers between devices, local(): lax.all_to_all(jnp.broadcast_to(reduced[None], (group_count,) + reduced.s...  18.9 us
    all_to_all x2, waiting for transfers between devices, local(): lax.all_to_all(weight_part, 'dp', split_axis=0, concat_axis=0, tiled=True)  17.3 us
    all_to_all x1, waiting for transfers between devices, local(): lax.all_to_all(jnp.broadcast_to(item_emb[None], (group_count, item_count,...  16.5 us
    all_to_all x2, starting transfers between devices, local(): lax.all_to_all(weight_part, 'dp', split_axis=0, concat_axis=0, tiled=True)  15.9 us
    all_gather x2, waiting for transfers between devices, local(): lax.all_gather(key_grad[:, k * part_width:(k + 1) * part_width], 'fsdp',...  12.5 us
  transfers between devices with their start and end apart: 10, of which 8 were waited for; matrix products, arithmetic and copies ran while one was open for 20% of the time, Pallas kernels for 0%

profile of v2, /device:TPU:6, one launch (start us, length us, event | category | flops | bytes accessed | tf_op | source)
XLA Modules:
  0.0 269.1 jit_solution(1439832048214023551)
XLA Ops:
  8.0 1.9 fusion.30
  10.6 0.9 fusion.27
  12.3 3.1 %multiply_reduce_fusion.1 = f32[512]{0:T(512)S(1)} fusion(bf16[512,4096]{1,0:T(8,128)(2,1)} %param.9), kind=kLoop, calls=%fused_computation.8 | loop fusion | flops 6290944 | bytes 4196352 | tf_op jit(solution)/shard_map/jvp()/reduce_sum | solution.py:10
  15.5 2.1 multiply_reduce_fusion
  17.7 1.0 broadcast_in_dim.24
  18.7 11.2 %all-to-all-start = ((bf16[16,4,4096]{2,1,0:T(4,128)(2,1)}), bf16[16,4,4096]{2,1,0:T(4,128)(2,1)S(1)}, u32[]{:S(2)}, u32[]{:S(2)}) async-start(bf16[16,4,4096]{2,1,0:T(4,128)(2,1)} %broadcast_in_dim.24), calls=%async_computation | async-start | bytes 1048576 | tf_op jit(solution)/shard_map/all_to_all | solution.py:58
  30.6 16.5 %all-to-all-done = bf16[16,4,4096]{2,1,0:T(4,128)(2,1)S(1)} async-done(((bf16[16,4,4096]{2,1,0:T(4,128)(2,1)}), bf16[16,4,4096]{2,1,0:T(4,128)(2,1)S(1)}, u32[]{:S(2)}, u32[]{:S(2)}) %all-to-all-start) | async-done | bytes 524320 | tf_op jit(solution)/shard_map/all_to_all | solution.py:58
  48.0 24.9 %all-gather.4.cloned.1.call-done = bf16[4096,1024]{1,0:T(8,128)(2,1)} async-done(((bf16[256,1024]{1,0:T(8,128)(2,1)}), bf16[4096,1024]{1,0:T(8,128)(2,1)}) %all-gather.4.cloned.1.call-update) | async-done | bytes 8388624 | tf_op jit(solution)/shard_map/all_gather | solution.py:44
  72.9 8.0 %fusion.10 = (f32[256]{0:T(256)S(1)}, f32[256]{0:T(256)S(1)}, f32[256,4096]{1,0:T(8,128)}) fusion(bf16[256,4096]{1,0:T(8,128)(2,1)S(1)} %convolution_convert_fusion, f32[4096]{0:T(1024)S(1)} %copy-done.7, bf16[256,1024]{1,0:T(8,128)(2,1)S(1)} %copy-done.5, bf16[4096,1024]{1,0:T(8,128)(2,1)} %all-gather.4.cloned.1.call-done), kind=kOutput, calls=%fused_computation.21 | convolution fusion | flops 2153774592 | bytes 15222784 | tf_op jit(solution)/shard_map/dot_general | solution.py:78
  81.7 1.3 copy-done.2
  83.0 1.6 copy.16
  84.5 4.8 %all-to-all-start.1 = ((bf16[16,256,256]{2,1,0:T(8,128)(2,1)}), bf16[16,256,256]{2,1,0:T(8,128)(2,1)}, u32[]{:S(2)}, u32[]{:S(2)}) async-start(bf16[16,256,256]{2,1,0:T(8,128)(2,1)} %bitcast.48), calls=%async_computation.1 | async-start | bytes 4194304 | tf_op jit(solution)/shard_map/all_to_all | solution.py:92
  89.3 3.3 %fusion.15 = f32[64,4096]{1,0:T(8,128)S(1)} fusion(bf16[256,4096]{1,0:T(8,128)(2,1)S(1)} %convolution_convert_fusion, f32[256,4096]{1,0:T(8,128)} %get-tuple-element.17, f32[256]{0:T(256)S(1)} %get-tuple-element.13, f32[256]{0:T(256)S(1)} %get-tuple-element.14, pred[256]{0:T(512)(128)(4,1)S(1)} %iota_compare_fusion.2, s32[256]{0:T(256)S(1)} %add.32), kind=kOutput, calls=%fused_computation.27 | convolution fusion | flops 141590528 | bytes 7343360 | tf_op jit(solution)/shard_map/dot_general | solution.py:83
  92.7 1.3 reshape.149
  93.9 33.4 %all-to-all-done.1 = bf16[16,256,256]{2,1,0:T(8,128)(2,1)} async-done(((bf16[16,256,256]{2,1,0:T(8,128)(2,1)}), bf16[16,256,256]{2,1,0:T(8,128)(2,1)}, u32[]{:S(2)}, u32[]{:S(2)}) %all-to-all-start.1) | async-done | bytes 2097184 | tf_op jit(solution)/shard_map/all_to_all | solution.py:92
  127.4 9.7 %all-to-all-start.2 = ((f32[16,4,4096]{2,1,0:T(4,128)}), f32[16,4,4096]{2,1,0:T(4,128)S(1)}, u32[]{:S(2)}, u32[]{:S(2)}) async-start(f32[16,4,4096]{2,1,0:T(4,128)} %reshape.149), calls=%async_computation.2 | async-start | bytes 2097152 | tf_op jit(solution)/shard_map/all_to_all | solution.py:87
  137.0 2.9 %copy.13 = bf16[256,4096]{1,0:T(8,128)(2,1)S(1)} copy(bf16[256,4096]{0,1:T(8,128)(2,1)} %bitcast.6) | data formatting | bytes 4194304 | tf_op jit(solution)/shard_map/dot_general | solution.py:98
  140.0 5.0 %fusion.11 = f32[16,16,512]{2,1,0:T(8,128)} fusion(bf16[16,16,4096]{2,1,0:T(8,128)(2,1)S(1)} %bitcast.49, bf16[4096,512]{1,0:T(8,128)(2,1)} %all-gather.8.cloned.1.call-done), kind=kOutput, calls=%fused_computation.22 | convolution fusion | flops 1073741824 | bytes 6815744 | tf_op jit(solution)/shard_map/dot_general | solution.py:98
  145.0 20.8 %all-to-all-done.2 = f32[16,4,4096]{2,1,0:T(4,128)S(1)} async-done(((f32[16,4,4096]{2,1,0:T(4,128)}), f32[16,4,4096]{2,1,0:T(4,128)S(1)}, u32[]{:S(2)}, u32[]{:S(2)}) %all-to-all-start.2) | async-done | bytes 1048608 | tf_op jit(solution)/shard_map/all_to_all | solution.py:87
  165.8 4.4 %all-to-all-start.5 = ((f32[16,16,512]{2,1,0:T(8,128)}), f32[16,16,512]{2,1,0:T(8,128)S(1)}, u32[]{:S(2)}, u32[]{:S(2)}) async-start(f32[16,16,512]{2,1,0:T(8,128)} %fusion.11), calls=%async_computation.5 | async-start | bytes 1048576 | tf_op jit(solution)/shard_map/all_to_all | solution.py:102
  170.3 12.5 %all-gather.6.cloned.1.call-done = bf16[4096,512]{1,0:T(8,128)(2,1)} async-done(((bf16[256,512]{1,0:T(8,128)(2,1)}), bf16[4096,512]{1,0:T(8,128)(2,1)}) %all-gather.6.cloned.1.call-update) | async-done | bytes 4194320 | tf_op jit(solution)/shard_map/all_gather | solution.py:48
  182.8 4.9 %fusion.13 = f32[16,16,512]{2,1,0:T(8,128)} fusion(bf16[16,16,4096]{2,1,0:T(8,128)(2,1)} %bitcast.50, bf16[4096,512]{1,0:T(8,128)(2,1)} %all-gather.6.cloned.1.call-done), kind=kOutput, calls=%fused_computation.24 | convolution fusion | flops 1073741824 | bytes 6815744 | tf_op jit(solution)/shard_map/dot_general | solution.py:98
  187.6 11.5 %all-to-all-start.3 = ((f32[16,16,512]{2,1,0:T(8,128)}), f32[16,16,512]{2,1,0:T(8,128)S(1)}, u32[]{:S(2)}, u32[]{:S(2)}) async-start(f32[16,16,512]{2,1,0:T(8,128)} %fusion.13), calls=%async_computation.3 | async-start | bytes 1048576 | tf_op jit(solution)/shard_map/all_to_all | solution.py:102
  199.2 17.3 %all-to-all-done.3 = f32[16,16,512]{2,1,0:T(8,128)S(1)} async-done(((f32[16,16,512]{2,1,0:T(8,128)}), f32[16,16,512]{2,1,0:T(8,128)S(1)}, u32[]{:S(2)}, u32[]{:S(2)}) %all-to-all-start.3) | async-done | bytes 524320 | tf_op jit(solution)/shard_map/all_to_all | solution.py:102
  217.4 4.8 %all-to-all-start.6 = ((f32[16,16,512]{2,1,0:T(8,128)}), f32[16,16,512]{2,1,0:T(8,128)S(1)}, u32[]{:S(2)}, u32[]{:S(2)}) async-start(f32[16,16,512]{2,1,0:T(8,128)} %broadcast_in_dim.29), calls=%async_computation.6 | async-start | bytes 1048576 | tf_op jit(solution)/shard_map/all_to_all | solution.py:108
  222.2 6.5 %convolution_convert_fusion.1 = bf16[256,1024]{1,0:T(8,128)(2,1)} fusion(bf16[256,4096]{1,0:T(8,128)(2,1)S(1)} %copy-done.3, bf16[4096,1024]{1,0:T(8,128)(2,1)} %all-gather.4.cloned.1.call-done), kind=kOutput, calls=%fused_computation.28 | convolution fusion | flops 2147745792 | bytes 11010048 | tf_op jit(solution)/shard_map/dot_general | solution.py:77
  228.7 10.6 %all-to-all-done.6 = f32[16,16,512]{2,1,0:T(8,128)S(1)} async-done(((f32[16,16,512]{2,1,0:T(8,128)}), f32[16,16,512]{2,1,0:T(8,128)S(1)}, u32[]{:S(2)}, u32[]{:S(2)}) %all-to-all-start.6) | async-done | bytes 524320 | tf_op jit(solution)/shard_map/all_to_all | solution.py:108
  240.1 4.8 %all-to-all-start.4 = ((f32[16,16,512]{2,1,0:T(8,128)}), f32[16,16,512]{2,1,0:T(8,128)S(1)}, u32[]{:S(2)}, u32[]{:S(2)}) async-start(f32[16,16,512]{2,1,0:T(8,128)} %broadcast_in_dim.28), calls=%async_computation.4 | async-start | bytes 1048576 | tf_op jit(solution)/shard_map/all_to_all | solution.py:108
  245.0 3.9 %fusion.4 = f32[512]{0:T(512)S(1)} fusion(bf16[512,4096]{1,0:T(8,128)(2,1)} %param.9, f32[4096]{0:T(1024)S(1)} %copy-done.6, f32[512]{0:T(512)S(1)} %get-tuple-element.15, f32[4,4096]{1,0:T(4,128)S(1)} %broadcast_divide_fusion), kind=kLoop, calls=%fused_computation.6 | loop fusion | flops 10485248 | bytes 4280320 | tf_op jit(solution)/shard_map/transpose(jvp())/reduce_sum | solution.py:10
  248.9 4.3 %fusion = bf16[512,4096]{1,0:T(8,128)(2,1)} fusion(bf16[512,4096]{1,0:T(8,128)(2,1)S(1)} %copy-done.1, f32[512]{0:T(512)S(1)} %multiply_multiply_fusion, f32[512]{0:T(512)S(1)} %get-tuple-element.11, f32[4096]{0:T(1024)S(1)} %copy-done.6, f32[512]{0:T(512)S(1)} %get-tuple-element.15, f32[4,4096]{1,0:T(4,128)S(1)} %broadcast_divide_fusion), kind=kLoop, calls=%fused_computation.1 | loop fusion | flops 16777216 | bytes 8476672 | tf_op jit(solution)/shard_map/convert_element_type | solution.py:118
  253.2 8.4 %all-to-all-done.4 = f32[16,16,512]{2,1,0:T(8,128)S(1)} async-done(((f32[16,16,512]{2,1,0:T(8,128)}), f32[16,16,512]{2,1,0:T(8,128)S(1)}, u32[]{:S(2)}, u32[]{:S(2)}) %all-to-all-start.4) | async-done | bytes 524320 | tf_op jit(solution)/shard_map/all_to_all | solution.py:108
  261.5 1.1 pad_maximum_fusion
  (44 shorter events, 6.2 us)
Async XLA Ops:
  7.2 8.3 %copy-start.6 = (f32[4096]{0:T(1024)S(1)}, f32[4096]{0:T(1024)}, u32[]{:S(2)}) copy-start(f32[4096]{0:T(1024)} %param.11) | copy-start | bytes 49156
  7.2 65.7 %all-gather.4.cloned.1.call-start = ((), (), s32[]{:S(2)}) async-start(), calls=%async_computation.7 | async-start | bytes 8912896 | tf_op jit(solution)/shard_map/all_gather | solution.py:44
  7.9 132.1 %all-gather.8.cloned.1.call-start = ((), (), s32[]{:S(2)}) async-start(), calls=%async_computation.9 | async-start | bytes 4456448 | tf_op jit(solution)/shard_map/all_gather | solution.py:48
  9.8 172.9 %all-gather.6.cloned.1.call-start = ((), (), s32[]{:S(2)}) async-start(), calls=%async_computation.8 | async-start | bytes 4456448 | tf_op jit(solution)/shard_map/all_gather | solution.py:48
  10.6 4.9 %copy-start = (bf16[512,4096]{1,0:T(8,128)(2,1)S(1)}, bf16[512,4096]{1,0:T(8,128)(2,1)}, u32[]{:S(2)}) copy-start(bf16[512,4096]{1,0:T(8,128)(2,1)} %param.9) | copy-start | bytes 12582916
  12.3 18.2 %copy-start.9 = (s32[256,1]{0,1:T(1,128)S(1)}, s32[256,1]{0,1:T(1,128)}, u32[]{:S(2)}) copy-start(s32[256,1]{0,1:T(1,128)} %param.12) | copy-start | bytes 3076
  12.3 18.2 %copy-start.8 = (s32[256]{0:T(256)S(1)}, s32[256]{0:T(256)}, u32[]{:S(2)}) copy-start(s32[256]{0:T(256)} %param.13) | copy-start | bytes 3076
  15.5 57.4 %copy-start.5 = (bf16[256,1024]{1,0:T(8,128)(2,1)S(1)}, bf16[256,1024]{1,0:T(8,128)(2,1)}, u32[]{:S(2)}) copy-start(bf16[256,1024]{1,0:T(8,128)(2,1)} %param.17) | copy-start | bytes 1572868
  15.5 57.4 %copy-start.7 = (f32[4096]{0:T(1024)S(1)}, f32[4096]{0:T(1024)}, u32[]{:S(2)}) copy-start(f32[4096]{0:T(1024)} %param.15) | copy-start | bytes 49156
  18.7 28.4 %all-to-all-start = ((bf16[16,4,4096]{2,1,0:T(4,128)(2,1)}), bf16[16,4,4096]{2,1,0:T(4,128)(2,1)S(1)}, u32[]{:S(2)}, u32[]{:S(2)}) async-start(bf16[16,4,4096]{2,1,0:T(4,128)(2,1)} %broadcast_in_dim.24), calls=%async_computation | async-start | bytes 1048576 | tf_op jit(solution)/shard_map/all_to_all | solution.py:58
  81.6 1.3 copy-start.2
  84.5 42.8 %all-to-all-start.1 = ((bf16[16,256,256]{2,1,0:T(8,128)(2,1)}), bf16[16,256,256]{2,1,0:T(8,128)(2,1)}, u32[]{:S(2)}, u32[]{:S(2)}) async-start(bf16[16,256,256]{2,1,0:T(8,128)(2,1)} %bitcast.48), calls=%async_computation.1 | async-start | bytes 4194304 | tf_op jit(solution)/shard_map/all_to_all | solution.py:92
  127.4 38.4 %all-to-all-start.2 = ((f32[16,4,4096]{2,1,0:T(4,128)}), f32[16,4,4096]{2,1,0:T(4,128)S(1)}, u32[]{:S(2)}, u32[]{:S(2)}) async-start(f32[16,4,4096]{2,1,0:T(4,128)} %reshape.149), calls=%async_computation.2 | async-start | bytes 2097152 | tf_op jit(solution)/shard_map/all_to_all | solution.py:87
  140.0 25.8 %copy-start.4 = (bf16[256,4096]{1,0:T(8,128)(2,1)}, bf16[256,4096]{1,0:T(8,128)(2,1)S(1)}, u32[]{:S(2)}) copy-start(bf16[256,4096]{1,0:T(8,128)(2,1)S(1)} %copy.13) | copy-start | bytes 6291460
  165.8 21.9 %all-to-all-start.5 = ((f32[16,16,512]{2,1,0:T(8,128)}), f32[16,16,512]{2,1,0:T(8,128)S(1)}, u32[]{:S(2)}, u32[]{:S(2)}) async-start(f32[16,16,512]{2,1,0:T(8,128)} %fusion.11), calls=%async_computation.5 | async-start | bytes 1048576 | tf_op jit(solution)/shard_map/all_to_all | solution.py:102
  170.3 51.9 %copy-start.3 = (bf16[256,4096]{1,0:T(8,128)(2,1)S(1)}, bf16[256,4096]{1,0:T(8,128)(2,1)}, u32[]{:S(2)}) copy-start(bf16[256,4096]{1,0:T(8,128)(2,1)} %copy-done.2) | copy-start | bytes 6291460
  187.6 28.9 %all-to-all-start.3 = ((f32[16,16,512]{2,1,0:T(8,128)}), f32[16,16,512]{2,1,0:T(8,128)S(1)}, u32[]{:S(2)}, u32[]{:S(2)}) async-start(f32[16,16,512]{2,1,0:T(8,128)} %fusion.13), calls=%async_computation.3 | async-start | bytes 1048576 | tf_op jit(solution)/shard_map/all_to_all | solution.py:102
  217.4 21.9 %all-to-all-start.6 = ((f32[16,16,512]{2,1,0:T(8,128)}), f32[16,16,512]{2,1,0:T(8,128)S(1)}, u32[]{:S(2)}, u32[]{:S(2)}) async-start(f32[16,16,512]{2,1,0:T(8,128)} %broadcast_in_dim.29), calls=%async_computation.6 | async-start | bytes 1048576 | tf_op jit(solution)/shard_map/all_to_all | solution.py:108
  240.1 21.4 %all-to-all-start.4 = ((f32[16,16,512]{2,1,0:T(8,128)}), f32[16,16,512]{2,1,0:T(8,128)S(1)}, u32[]{:S(2)}, u32[]{:S(2)}) async-start(f32[16,16,512]{2,1,0:T(8,128)} %broadcast_in_dim.28), calls=%async_computation.4 | async-start | bytes 1048576 | tf_op jit(solution)/shard_map/all_to_all | solution.py:108
  244.9 4.0 %copy-start.1 = (bf16[512,4096]{1,0:T(8,128)(2,1)S(1)}, bf16[512,4096]{1,0:T(8,128)(2,1)}, u32[]{:S(2)}) copy-start(bf16[512,4096]{1,0:T(8,128)(2,1)} %param.9) | copy-start | bytes 12582916
Sparse Core Ops, SparseCore 0:
  9.8 63.0 all-gather.3
  74.7 60.0 all-gather.7
  136.7 46.0 all-gather.5

commit v3 on v1

--- a/solution.py
+++ b/solution.py
@@ -41,8 +41,13 @@
 
     pooled, pool_back = jax.vjp(pooling, stacked_tokens.astype(jnp.float32))
     item_emb = pooled.astype(jnp.bfloat16)
-    weights = lax.all_gather(key_weight, "fsdp", axis=0, tiled=True)
-    grads_all = lax.all_gather(key_grad, "fsdp", axis=0, tiled=True)
+    fsdp_count = lax.axis_size("fsdp")
+    shard_rows = key_weight.shape[0]
+    gathered = lax.all_gather(
+        jnp.concatenate([key_weight, key_grad], axis=0), "fsdp", axis=0, tiled=False
+    )
+    weights = gathered[:, :shard_rows].reshape(fsdp_count * shard_rows, key_weight.shape[1])
+    grads_all = gathered[:, shard_rows:].reshape(fsdp_count * key_grad.shape[0], key_grad.shape[1])
     row_count = user_slot.shape[0]
     source = user_source[:, 0]
     seq_count = user_lengths.shape[0]
@@ -75,30 +80,35 @@
     )
     (embed_grad,) = norm_back(hidden_grad)
     pos_grad = jnp.where(alive_mask, embed_grad, jnp.zeros_like(embed_grad)).astype(jnp.bfloat16)
-    hidden_cols = lax.all_to_all(hidden, "fsdp", split_axis=1, concat_axis=0, tiled=True)
+    hidden_split = hidden.reshape(row_count, fsdp_count, model_width // fsdp_count).transpose(1, 0, 2)
+    hidden_cols = lax.all_to_all(hidden_split, "fsdp", split_axis=0, concat_axis=0, tiled=True).reshape(
+        fsdp_count * row_count, model_width // fsdp_count
+    )
     weight_part = lax.dot_general(
         hidden_cols, grads_all, (((0,), (0,)), ((), ())), preferred_element_type=jnp.float32
     )
-    weight_rows = weight_part.shape[0]
-    reduced = jnp.sum(
-        lax.all_to_all(weight_part, "dp", split_axis=0, concat_axis=0, tiled=True).reshape(
-            group_count, weight_rows // group_count, weight_part.shape[1]
-        ),
-        axis=0,
+    weight_rows, weight_cols = weight_part.shape
+    item_part = lax.dot_general(
+        pick, pos_grad, (((0,), (0,)), ((), ())), preferred_element_type=jnp.float32
     )
+    item_rows = item_count * model_width // weight_cols
+    outgoing = jnp.concatenate(
+        [
+            weight_part.reshape(group_count, weight_rows // group_count, weight_cols),
+            item_part.reshape(group_count, item_rows, weight_cols),
+        ],
+        axis=1,
+    )
+    arrived = jnp.sum(lax.all_to_all(outgoing, "dp", split_axis=0, concat_axis=0, tiled=True), axis=0)
+    reduced = arrived[: weight_rows // group_count]
+    item_grad = arrived[weight_rows // group_count :].reshape(item_count, model_width)
     weight_grad = lax.all_to_all(
         jnp.broadcast_to(reduced[None], (group_count,) + reduced.shape),
         "dp",
         split_axis=0,
         concat_axis=0,
         tiled=True,
-    ).reshape(weight_rows, weight_part.shape[1])
-    item_part = lax.dot_general(
-        pick, pos_grad, (((0,), (0,)), ((), ())), preferred_element_type=jnp.float32
-    ).reshape(group_count, item_count, model_width)
-    item_grad = jnp.sum(
-        lax.all_to_all(item_part, "dp", split_axis=0, concat_axis=0, tiled=True), axis=0
-    )
+    ).reshape(weight_rows, weight_cols)
     (tokens_back,) = pool_back(item_grad)
     token_grads = tokens_back.reshape(item_count * block_rows, model_width).astype(jnp.bfloat16)
     return (key_rows, weight_grad, token_grads)

time: 275 us -> 277 us (level)
  blocking collectives: 48.6 us -> 60.5 us
  local copies, waits for them, and re-layouts: 9.04 us -> 18.9 us
  waiting for transfers between devices: 127 us -> 118 us
  starting transfers between devices: 29.5 us -> 21 us
  matrix products: 25.8 us -> 21 us
    all_to_all x2 -> x1, waiting for transfers between devices: 52.1 us -> 21.6 us  [local(): lax.all_to_all(hidden_split, 'fsdp', split_axis=0, concat_axis=0, tiled=T...]
    all_gather x2 -> x1, waiting for transfers between devices: 44.6 us -> 66.1 us  [local(): lax.all_gather(jnp.concatenate([key_weight, key_grad], axis=0), 'fsdp', a...]
    all_to_all x1, blocking collectives: 48.6 us -> 60.5 us  [local(): lax.all_to_all(outgoing, 'dp', split_axis=0, concat_axis=0, tiled=True)]
    slice x0 -> x2, local copies, waits for them, and re-layouts: none -> 9.58 us  [the longest x1 9.57 us: local(): gathered[:, shard_rows:]]
    all_to_all x2 -> x1, starting transfers between devices: 13.9 us -> 4.91 us  [local(): lax.all_to_all(hidden_split, 'fsdp', split_axis=0, concat_axis=0, tiled=T...]
    dot_general x1, matrix products: 7.97 us -> 4.77 us  [local(): lax.dot_general(key_grad, weights, (((1,), (1,)), ((), ())), preferred_el...]
  transfers between devices with their start and end apart: 6 -> 4, of which waited for: 6 -> 4; matrix products, arithmetic and copies ran while one was open for 16% -> 10% of each run, Pallas kernels for 0% -> 0%
where the time goes in v3:
time: 277 us; the launch traced here: 275 us
  waiting for transfers between devices  118 us (43%)
  blocking collectives  60.5 us (22%)
  starting transfers between devices  21 us (8%)
  matrix products  21 us (8%)
  other arithmetic  20.1 us (7%)
  local copies, waits for them, and re-layouts  18.9 us (7%)
  between operations  14.9 us (5%)
    all_gather x1, waiting for transfers between devices, local(): lax.all_gather(jnp.concatenate([key_weight, key_grad], axis=0), 'fsdp', a...  66.1 us
    all_to_all x1, blocking collectives, local(): lax.all_to_all(outgoing, 'dp', split_axis=0, concat_axis=0, tiled=True)  60.5 us
    all_to_all x1, waiting for transfers between devices, local(): lax.all_to_all(hidden_split, 'fsdp', split_axis=0, concat_axis=0, tiled=T...  21.6 us
    all_to_all x1, waiting for transfers between devices, local(): lax.all_to_all(jnp.broadcast_to(item_emb[None], (group_count, item_count,...  16.5 us
    all_to_all x1, waiting for transfers between devices, local(): lax.all_to_all(jnp.broadcast_to(reduced[None], (group_count,) + reduced.s...  14 us
    all_to_all x1, starting transfers between devices, local(): lax.all_to_all(jnp.broadcast_to(item_emb[None], (group_count, item_count,...  11.2 us
    slice x1, local copies, waits for them, and re-layouts, local(): gathered[:, shard_rows:]  9.57 us
    dot_general x1, matrix products, local(): jnp.dot(hidden, weights, preferred_element_type=jnp.float32)  6.5 us
  transfers between devices with their start and end apart: 4, of which 4 were waited for; matrix products, arithmetic and copies ran while one was open for 10% of the time, Pallas kernels for 0%

profile of v3, /device:TPU:6, one launch (start us, length us, event | category | flops | bytes accessed | tf_op | source)
XLA Modules:
  0.0 274.6 jit_solution(6658721044223647321)
XLA Ops:
  7.2 2.2 pad_maximum_fusion.1
  9.5 0.8 convert_element_type.57
  10.3 0.9 fusion.24
  11.2 3.1 %multiply_reduce_fusion.1 = f32[512]{0:T(512)S(1)} fusion(bf16[512,4096]{1,0:T(8,128)(2,1)} %param.9), kind=kLoop, calls=%fused_computation.8 | loop fusion | flops 6290944 | bytes 4196352 | tf_op jit(solution)/shard_map/jvp()/reduce_sum | solution.py:10
  14.3 2.1 multiply_reduce_fusion
  16.5 1.0 broadcast_in_dim.22
  17.5 11.2 %all-to-all-start = ((bf16[16,4,4096]{2,1,0:T(4,128)(2,1)}), bf16[16,4,4096]{2,1,0:T(4,128)(2,1)S(1)}, u32[]{:S(2)}, u32[]{:S(2)}) async-start(bf16[16,4,4096]{2,1,0:T(4,128)(2,1)} %broadcast_in_dim.22), calls=%async_computation | async-start | bytes 1048576 | tf_op jit(solution)/shard_map/all_to_all | solution.py:58
  29.5 16.5 %all-to-all-done = bf16[16,4,4096]{2,1,0:T(4,128)(2,1)S(1)} async-done(((bf16[16,4,4096]{2,1,0:T(4,128)(2,1)}), bf16[16,4,4096]{2,1,0:T(4,128)(2,1)S(1)}, u32[]{:S(2)}, u32[]{:S(2)}) %all-to-all-start) | async-done | bytes 524320 | tf_op jit(solution)/shard_map/all_to_all | solution.py:58
  45.9 0.1 reshape.143
  46.1 0.8 convolution_convert_fusion
  46.8 66.1 %all-gather.3.cloned.1.call-done = bf16[8192,1024]{1,0:T(8,128)(2,1)} async-done(((bf16[512,1024]{1,0:T(8,128)(2,1)}), bf16[8192,1024]{1,0:T(8,128)(2,1)}) %all-gather.3.cloned.1.call-update) | async-done | bytes 16777232 | tf_op jit(solution)/shard_map/all_gather | solution.py:46
  112.9 9.6 %fusion.27 = (bf16[16,256,1024]{2,1,0:T(8,128)(2,1)}, bf16[16,256,1024]{2,1,0:T(8,128)(2,1)S(1)}) fusion(bf16[16,512,1024]{2,1,0:T(8,128)(2,1)} %bitcast.47), kind=kLoop, calls=%fused_computation.49 | loop fusion | bytes 33554432 | tf_op jit(solution)/shard_map/slice | solution.py:50
  122.5 4.8 %fusion.11 = (f32[256]{0:T(256)S(1)}, f32[256]{0:T(256)S(1)}, f32[256,4096]{1,0:T(8,128)}) fusion(bf16[256,4096]{1,0:T(8,128)(2,1)S(1)} %convolution_convert_fusion, f32[4096]{0:T(1024)S(1)} %copy-done.7, bf16[4096,1024]{1,0:T(8,128)(2,1)S(1)} %bitcast.50, bf16[256,1024]{1,0:T(8,128)(2,1)S(1)} %copy-done.5), kind=kOutput, calls=%fused_computation.22 | convolution fusion | flops 2153774592 | bytes 15222784 | tf_op jit(solution)/shard_map/dot_general | solution.py:78
  127.2 0.7 fusion.10
  128.0 1.3 copy-done.2
  129.4 1.5 copy.19
  130.9 4.9 %all-to-all-start.1 = ((bf16[16,256,256]{2,1,0:T(8,128)(2,1)}), bf16[16,256,256]{2,1,0:T(8,128)(2,1)}, u32[]{:S(2)}, u32[]{:S(2)}) async-start(bf16[16,256,256]{2,1,0:T(8,128)(2,1)} %bitcast.49), calls=%async_computation.1 | async-start | bytes 4194304 | tf_op jit(solution)/shard_map/all_to_all | solution.py:84
  135.8 3.3 %fusion.12 = f32[64,4096]{1,0:T(8,128)S(1)} fusion(bf16[256,4096]{1,0:T(8,128)(2,1)S(1)} %convolution_convert_fusion, f32[256,4096]{1,0:T(8,128)} %get-tuple-element.15, f32[256]{0:T(256)S(1)} %get-tuple-element.11, f32[256]{0:T(256)S(1)} %get-tuple-element.12, pred[256]{0:T(512)(128)(4,1)S(1)} %iota_compare_fusion.2, s32[256]{0:T(256)S(1)} %add.32), kind=kOutput, calls=%fused_computation.25 | convolution fusion | flops 141590528 | bytes 7343360 | tf_op jit(solution)/shard_map/dot_general | solution.py:91
  139.1 0.3 reshape.148
  139.4 21.6 %all-to-all-done.1 = bf16[16,256,256]{2,1,0:T(8,128)(2,1)} async-done(((bf16[16,256,256]{2,1,0:T(8,128)(2,1)}), bf16[16,256,256]{2,1,0:T(8,128)(2,1)}, u32[]{:S(2)}, u32[]{:S(2)}) %all-to-all-start.1) | async-done | bytes 2097184 | tf_op jit(solution)/shard_map/all_to_all | solution.py:84
  161.0 2.9 %copy.14 = bf16[256,4096]{1,0:T(8,128)(2,1)S(1)} copy(bf16[256,4096]{0,1:T(8,128)(2,1)} %bitcast.8) | data formatting | bytes 4194304 | tf_op jit(solution)/shard_map/dot_general | solution.py:87
  163.9 5.7 %fusion.29 = f32[16,16,1024]{2,1,0:T(8,128)S(1)} fusion(bf16[16,16,4096]{2,1,0:T(8,128)(2,1)S(1)} %bitcast.54, bf16[4096,1024,1]{1,0,2:T(8,128)(2,1)} %bitcast.52), kind=kOutput, calls=%fused_computation.51 | convolution fusion | flops 2147483648 | bytes 11534336 | tf_op jit(solution)/shard_map/dot_general | solution.py:87
  169.6 0.2 pad_maximum_fusion
  169.8 60.5 %all_to_all.20 = f32[16,32,1024]{2,1,0:T(8,128)} all-to-all(f32[16,32,1024]{2,1,0:T(8,128)S(1)} %pad_maximum_fusion), channel_id=1, replica_groups=mesh['dp'=16,'fsdp'=16] {'dp'}, dimensions={0} | all-to-all | bytes 4194304 | tf_op jit(solution)/shard_map/all_to_all | solution.py:102
  230.3 1.7 reduce_sum.66
  232.0 1.1 broadcast_in_dim.26
  233.1 4.8 %all-to-all-start.3 = ((f32[16,16,1024]{2,1,0:T(8,128)}), f32[16,16,1024]{2,1,0:T(8,128)S(1)}, u32[]{:S(2)}, u32[]{:S(2)}) async-start(f32[16,16,1024]{2,1,0:T(8,128)} %broadcast_in_dim.26), calls=%async_computation.3 | async-start | bytes 2097152 | tf_op jit(solution)/shard_map/all_to_all | solution.py:105
  238.0 6.5 %convolution_convert_fusion.1 = bf16[256,1024]{1,0:T(8,128)(2,1)} fusion(bf16[256,4096]{1,0:T(8,128)(2,1)S(1)} %copy-done.3, bf16[4096,1024]{1,0:T(8,128)(2,1)} %bitcast.51), kind=kOutput, calls=%fused_computation.26 | convolution fusion | flops 2147745792 | bytes 11010048 | tf_op jit(solution)/shard_map/dot_general | solution.py:77
  244.6 3.9 %fusion.4 = f32[512]{0:T(512)S(1)} fusion(bf16[512,4096]{1,0:T(8,128)(2,1)} %param.9, f32[4096]{0:T(1024)S(1)} %copy-done.6, f32[512]{0:T(512)S(1)} %get-tuple-element.13, f32[4,4096]{1,0:T(4,128)S(1)} %broadcast_divide_fusion), kind=kLoop, calls=%fused_computation.6 | loop fusion | flops 10485248 | bytes 4280320 | tf_op jit(solution)/shard_map/transpose(jvp())/reduce_sum | solution.py:10
  248.5 4.3 %fusion = bf16[512,4096]{1,0:T(8,128)(2,1)} fusion(bf16[512,4096]{1,0:T(8,128)(2,1)S(1)} %copy-done.1, f32[512]{0:T(512)S(1)} %multiply_multiply_fusion, f32[512]{0:T(512)S(1)} %get-tuple-element.9, f32[4096]{0:T(1024)S(1)} %copy-done.6, f32[512]{0:T(512)S(1)} %get-tuple-element.13, f32[4,4096]{1,0:T(4,128)S(1)} %broadcast_divide_fusion), kind=kLoop, calls=%fused_computation.1 | loop fusion | flops 16777216 | bytes 8476672 | tf_op jit(solution)/shard_map/convert_element_type | solution.py:113
  252.8 14.0 %all-to-all-done.3 = f32[16,16,1024]{2,1,0:T(8,128)S(1)} async-done(((f32[16,16,1024]{2,1,0:T(8,128)}), f32[16,16,1024]{2,1,0:T(8,128)S(1)}, u32[]{:S(2)}, u32[]{:S(2)}) %all-to-all-start.3) | async-done | bytes 1048608 | tf_op jit(solution)/shard_map/all_to_all | solution.py:105
  266.8 1.0 copy.22
  (31 shorter events, 0.4 us)
Async XLA Ops:
  7.2 7.2 %copy-start.6 = (f32[4096]{0:T(1024)S(1)}, f32[4096]{0:T(1024)}, u32[]{:S(2)}) copy-start(f32[4096]{0:T(1024)} %param.11) | copy-start | bytes 49156
  7.2 105.7 %all-gather.3.cloned.1.call-start = ((), (), s32[]{:S(2)}) async-start(), calls=%async_computation.4 | async-start | bytes 17825792 | tf_op jit(solution)/shard_map/all_gather | solution.py:46
  9.5 4.9 %copy-start = (bf16[512,4096]{1,0:T(8,128)(2,1)S(1)}, bf16[512,4096]{1,0:T(8,128)(2,1)}, u32[]{:S(2)}) copy-start(bf16[512,4096]{1,0:T(8,128)(2,1)} %param.9) | copy-start | bytes 12582916
  11.2 18.2 %copy-start.9 = (s32[256,1]{0,1:T(1,128)S(1)}, s32[256,1]{0,1:T(1,128)}, u32[]{:S(2)}) copy-start(s32[256,1]{0,1:T(1,128)} %param.12) | copy-start | bytes 3076
  11.2 18.2 %copy-start.8 = (s32[256]{0:T(256)S(1)}, s32[256]{0:T(256)}, u32[]{:S(2)}) copy-start(s32[256]{0:T(256)} %param.13) | copy-start | bytes 3076
  17.5 28.4 %all-to-all-start = ((bf16[16,4,4096]{2,1,0:T(4,128)(2,1)}), bf16[16,4,4096]{2,1,0:T(4,128)(2,1)S(1)}, u32[]{:S(2)}, u32[]{:S(2)}) async-start(bf16[16,4,4096]{2,1,0:T(4,128)(2,1)} %broadcast_in_dim.22), calls=%async_computation | async-start | bytes 1048576 | tf_op jit(solution)/shard_map/all_to_all | solution.py:58
  112.9 9.6 %copy-start.5 = (bf16[256,1024]{1,0:T(8,128)(2,1)S(1)}, bf16[256,1024]{1,0:T(8,128)(2,1)}, u32[]{:S(2)}) copy-start(bf16[256,1024]{1,0:T(8,128)(2,1)} %param.17) | copy-start | bytes 1572868
  112.9 9.6 %copy-start.7 = (f32[4096]{0:T(1024)S(1)}, f32[4096]{0:T(1024)}, u32[]{:S(2)}) copy-start(f32[4096]{0:T(1024)} %param.15) | copy-start | bytes 49156
  122.5 4.8 %copy-start.4 = (bf16[16,256,1024]{2,1,0:T(8,128)(2,1)}, bf16[16,256,1024]{2,1,0:T(8,128)(2,1)S(1)}, u32[]{:S(2)}) copy-start(bf16[16,256,1024]{2,1,0:T(8,128)(2,1)S(1)} %get-tuple-element.6) | copy-start | bytes 25165828
  128.0 1.4 copy-start.2
  130.9 30.1 %all-to-all-start.1 = ((bf16[16,256,256]{2,1,0:T(8,128)(2,1)}), bf16[16,256,256]{2,1,0:T(8,128)(2,1)}, u32[]{:S(2)}, u32[]{:S(2)}) async-start(bf16[16,256,256]{2,1,0:T(8,128)(2,1)} %bitcast.49), calls=%async_computation.1 | async-start | bytes 4194304 | tf_op jit(solution)/shard_map/all_to_all | solution.py:84
  169.8 68.1 %copy-start.3 = (bf16[256,4096]{1,0:T(8,128)(2,1)S(1)}, bf16[256,4096]{1,0:T(8,128)(2,1)}, u32[]{:S(2)}) copy-start(bf16[256,4096]{1,0:T(8,128)(2,1)} %copy-done.2) | copy-start | bytes 6291460
  233.1 33.6 %all-to-all-start.3 = ((f32[16,16,1024]{2,1,0:T(8,128)}), f32[16,16,1024]{2,1,0:T(8,128)S(1)}, u32[]{:S(2)}, u32[]{:S(2)}) async-start(f32[16,16,1024]{2,1,0:T(8,128)} %broadcast_in_dim.26), calls=%async_computation.3 | async-start | bytes 2097152 | tf_op jit(solution)/shard_map/all_to_all | solution.py:105
  244.5 4.0 %copy-start.1 = (bf16[512,4096]{1,0:T(8,128)(2,1)S(1)}, bf16[512,4096]{1,0:T(8,128)(2,1)}, u32[]{:S(2)}) copy-start(bf16[512,4096]{1,0:T(8,128)(2,1)} %param.9) | copy-start | bytes 12582916
Sparse Core Ops, SparseCore 0:
  10.4 102.4 all-gather.2

commit v4 on v3

--- a/solution.py
+++ b/solution.py
@@ -74,16 +74,17 @@
 
     scaled, norm_back = jax.vjp(normalize, embedded.astype(jnp.float32))
     hidden = scaled.astype(jnp.bfloat16)
+    hidden_split = hidden.reshape(row_count, fsdp_count, model_width // fsdp_count).transpose(1, 0, 2)
+    hidden_cols = lax.all_to_all(hidden_split, "fsdp", split_axis=0, concat_axis=0, tiled=True).reshape(
+        fsdp_count * row_count, model_width // fsdp_count
+    )
     key_rows = jnp.dot(hidden, weights, preferred_element_type=jnp.float32).astype(jnp.bfloat16)
     hidden_grad = lax.dot_general(
         key_grad, weights, (((1,), (1,)), ((), ())), preferred_element_type=jnp.float32
     )
     (embed_grad,) = norm_back(hidden_grad)
     pos_grad = jnp.where(alive_mask, embed_grad, jnp.zeros_like(embed_grad)).astype(jnp.bfloat16)
-    hidden_split = hidden.reshape(row_count, fsdp_count, model_width // fsdp_count).transpose(1, 0, 2)
-    hidden_cols = lax.all_to_all(hidden_split, "fsdp", split_axis=0, concat_axis=0, tiled=True).reshape(
-        fsdp_count * row_count, model_width // fsdp_count
-    )
+    hidden_cols, weights, grads_all = lax.optimization_barrier((hidden_cols, weights, grads_all))
     weight_part = lax.dot_general(
         hidden_cols, grads_all, (((0,), (0,)), ((), ())), preferred_element_type=jnp.float32
     )
@@ -98,8 +99,10 @@
             item_part.reshape(group_count, item_rows, weight_cols),
         ],
         axis=1,
+    ).astype(jnp.bfloat16)
+    arrived = jnp.sum(
+        lax.all_to_all(outgoing, "dp", split_axis=0, concat_axis=0, tiled=True).astype(jnp.float32), axis=0
     )
-    arrived = jnp.sum(lax.all_to_all(outgoing, "dp", split_axis=0, concat_axis=0, tiled=True), axis=0)
     reduced = arrived[: weight_rows // group_count]
     item_grad = arrived[weight_rows // group_count :].reshape(item_count, model_width)
     weight_grad = lax.all_to_all(

time: 277 us -> 250 us (0.903)
  blocking collectives: 60.5 us -> 38 us
  local copies, waits for them, and re-layouts: 18.9 us -> 16 us
    all_to_all x1, blocking collectives: 60.5 us -> 38 us  [local(): lax.all_to_all(outgoing, 'dp', split_axis=0, concat_axis=0, tiled=True)]
    dot_general x1 -> x0, local copies, waits for them, and re-layouts: 2.91 us -> none  [local(): lax.dot_general(hidden_cols, grads_all, (((0,), (0,)), ((), ())), preferr...]
  transfers between devices with their start and end apart: 4 -> 4, of which waited for: 4 -> 4; matrix products, arithmetic and copies ran while one was open for 10% -> 11% of each run, Pallas kernels for 0% -> 0%
where the time goes in v4:
time: 250 us; the launch traced here: 247 us
  waiting for transfers between devices  117 us (47%)
  blocking collectives  38 us (15%)
  matrix products  21.7 us (9%)
  starting transfers between devices  20.7 us (8%)
  other arithmetic  18.5 us (7%)
  local copies, waits for them, and re-layouts  16 us (6%)
  between operations  14.9 us (6%)
    all_gather x1, waiting for transfers between devices, local(): lax.all_gather(jnp.concatenate([key_weight, key_grad], axis=0), 'fsdp', a...  66.1 us
    all_to_all x1, blocking collectives, local(): lax.all_to_all(outgoing, 'dp', split_axis=0, concat_axis=0, tiled=True)  38 us
    all_to_all x1, waiting for transfers between devices, local(): lax.all_to_all(hidden_split, 'fsdp', split_axis=0, concat_axis=0, tiled=T...  21.1 us
    all_to_all x1, waiting for transfers between devices, local(): lax.all_to_all(jnp.broadcast_to(item_emb[None], (group_count, item_count,...  16.5 us
    all_to_all x1, waiting for transfers between devices, local(): lax.all_to_all(jnp.broadcast_to(reduced[None], (group_count,) + reduced.s...  13.9 us
    all_to_all x1, starting transfers between devices, local(): lax.all_to_all(jnp.broadcast_to(item_emb[None], (group_count, item_count,...  11.2 us
    slice x1, local copies, waits for them, and re-layouts, local(): gathered[:, shard_rows:]  9.56 us
    dot_general x1, matrix products, local(): jnp.dot(hidden, weights, preferred_element_type=jnp.float32)  6.5 us
  transfers between devices with their start and end apart: 4, of which 4 were waited for; matrix products, arithmetic and copies ran while one was open for 11% of the time, Pallas kernels for 0%

profile of v4, /device:TPU:6, one launch (start us, length us, event | category | flops | bytes accessed | tf_op | source)
XLA Modules:
  0.0 247.2 jit_solution(8364545200702711404)
XLA Ops:
  7.2 2.2 pad_maximum_fusion
  9.5 0.8 convert_element_type.61
  10.3 0.9 fusion.27
  11.2 3.1 %multiply_reduce_fusion.1 = f32[512]{0:T(512)S(1)} fusion(bf16[512,4096]{1,0:T(8,128)(2,1)} %param.9), kind=kLoop, calls=%fused_computation.8 | loop fusion | flops 6290944 | bytes 4196352 | tf_op jit(solution)/shard_map/jvp()/reduce_sum | solution.py:10
  14.3 2.1 multiply_reduce_fusion
  16.5 0.1 divide_convert_fusion
  16.5 1.0 broadcast_in_dim.22
  17.5 11.2 %all-to-all-start = ((bf16[16,4,4096]{2,1,0:T(4,128)(2,1)}), bf16[16,4,4096]{2,1,0:T(4,128)(2,1)S(1)}, u32[]{:S(2)}, u32[]{:S(2)}) async-start(bf16[16,4,4096]{2,1,0:T(4,128)(2,1)} %broadcast_in_dim.22), calls=%async_computation | async-start | bytes 1048576 | tf_op jit(solution)/shard_map/all_to_all | solution.py:58
  29.5 16.5 %all-to-all-done = bf16[16,4,4096]{2,1,0:T(4,128)(2,1)S(1)} async-done(((bf16[16,4,4096]{2,1,0:T(4,128)(2,1)}), bf16[16,4,4096]{2,1,0:T(4,128)(2,1)S(1)}, u32[]{:S(2)}, u32[]{:S(2)}) %all-to-all-start) | async-done | bytes 524320 | tf_op jit(solution)/shard_map/all_to_all | solution.py:58
  45.9 0.1 reshape.146
  46.1 0.8 convolution_convert_fusion
  46.8 66.1 %all-gather.3.cloned.1.call-done = bf16[8192,1024]{1,0:T(8,128)(2,1)} async-done(((bf16[512,1024]{1,0:T(8,128)(2,1)}), bf16[8192,1024]{1,0:T(8,128)(2,1)}) %all-gather.3.cloned.1.call-update) | async-done | bytes 16777232 | tf_op jit(solution)/shard_map/all_gather | solution.py:46
  112.9 9.6 %fusion.30 = (bf16[16,256,1024]{2,1,0:T(8,128)(2,1)}, bf16[16,256,1024]{2,1,0:T(8,128)(2,1)S(1)}) fusion(bf16[16,512,1024]{2,1,0:T(8,128)(2,1)} %bitcast.44), kind=kLoop, calls=%fused_computation.55 | loop fusion | bytes 33554432 | tf_op jit(solution)/shard_map/slice | solution.py:50
  122.5 4.8 %fusion.11 = (f32[256]{0:T(256)S(1)}, f32[256]{0:T(256)S(1)}, f32[256,4096]{1,0:T(8,128)}) fusion(bf16[256,4096]{1,0:T(8,128)(2,1)S(1)} %convolution_convert_fusion, f32[4096]{0:T(1024)S(1)} %copy-done.8, bf16[4096,1024]{1,0:T(8,128)(2,1)S(1)} %bitcast.48, bf16[256,1024]{1,0:T(8,128)(2,1)S(1)} %copy-done.6), kind=kOutput, calls=%fused_computation.23 | convolution fusion | flops 2153774592 | bytes 15222784 | tf_op jit(solution)/shard_map/dot_general | solution.py:82
  127.2 0.7 fusion.10
  128.0 1.4 copy-done.2
  129.4 1.5 copy.18
  130.9 4.7 %all-to-all-start.1 = ((bf16[16,256,256]{2,1,0:T(8,128)(2,1)}), bf16[16,256,256]{2,1,0:T(8,128)(2,1)S(1)}, u32[]{:S(2)}, u32[]{:S(2)}) async-start(bf16[16,256,256]{2,1,0:T(8,128)(2,1)} %bitcast.47), calls=%async_computation.1 | async-start | bytes 4194304 | tf_op jit(solution)/shard_map/all_to_all | solution.py:78
  135.6 3.9 %convolution_convert_fusion.1 = bf16[64,4096]{1,0:T(8,128)(2,1)S(1)} fusion(bf16[256,4096]{1,0:T(8,128)(2,1)} %copy-done.4, f32[256,4096]{1,0:T(8,128)} %get-tuple-element.19, f32[256]{0:T(256)S(1)} %get-tuple-element.15, f32[256]{0:T(256)S(1)} %get-tuple-element.16, pred[256]{0:T(512)(128)(4,1)S(1)} %iota_compare_fusion.2, s32[256]{0:T(256)S(1)} %add.32), kind=kOutput, calls=%fused_computation.17 | convolution fusion | flops 141852672 | bytes 6819072 | tf_op jit(solution)/shard_map/dot_general | solution.py:92
  139.5 0.3 reshape.152
  139.8 21.1 %all-to-all-done.1 = bf16[16,256,256]{2,1,0:T(8,128)(2,1)S(1)} async-done(((bf16[16,256,256]{2,1,0:T(8,128)(2,1)}), bf16[16,256,256]{2,1,0:T(8,128)(2,1)S(1)}, u32[]{:S(2)}, u32[]{:S(2)}) %all-to-all-start.1) | async-done | bytes 2097184 | tf_op jit(solution)/shard_map/all_to_all | solution.py:78
  160.9 5.7 %convolution_convert_fusion.2 = bf16[256,1024]{1,0:T(8,128)(2,1)S(1)} fusion(bf16[4096,256]{1,0:T(8,128)(2,1)S(1)} %bitcast.45, bf16[4096,1024]{1,0:T(8,128)(2,1)} %bitcast.43), kind=kOutput, calls=%fused_computation.30 | convolution fusion | flops 2147745792 | bytes 11010048 | tf_op jit(solution)/shard_map/dot_general | solution.py:88
  166.6 0.1 pad_maximum_fusion.1
  166.7 38.0 %all_to_all.20 = bf16[16,32,1024]{2,1,0:T(8,128)(2,1)S(1)} all-to-all(bf16[16,32,1024]{2,1,0:T(8,128)(2,1)S(1)} %pad_maximum_fusion.1), channel_id=1, replica_groups=mesh['dp'=16,'fsdp'=16] {'dp'}, dimensions={0} | all-to-all | bytes 2097152 | tf_op jit(solution)/shard_map/all_to_all | solution.py:104
  204.7 0.2 convert_reduce_fusion
  204.9 1.1 broadcast_in_dim.26
  206.0 4.8 %all-to-all-start.3 = ((f32[16,16,1024]{2,1,0:T(8,128)}), f32[16,16,1024]{2,1,0:T(8,128)S(1)}, u32[]{:S(2)}, u32[]{:S(2)}) async-start(f32[16,16,1024]{2,1,0:T(8,128)} %broadcast_in_dim.26), calls=%async_computation.3 | async-start | bytes 2097152 | tf_op jit(solution)/shard_map/all_to_all | solution.py:108
  210.8 6.5 %convolution_convert_fusion.3 = bf16[256,1024]{1,0:T(8,128)(2,1)} fusion(bf16[256,4096]{1,0:T(8,128)(2,1)S(1)} %copy-done.3, bf16[4096,1024]{1,0:T(8,128)(2,1)} %bitcast.49), kind=kOutput, calls=%fused_computation.31 | convolution fusion | flops 2147745792 | bytes 11010048 | tf_op jit(solution)/shard_map/dot_general | solution.py:81
  217.4 3.9 %fusion.4 = f32[512]{0:T(512)S(1)} fusion(bf16[512,4096]{1,0:T(8,128)(2,1)} %param.9, f32[4096]{0:T(1024)S(1)} %copy-done.7, f32[512]{0:T(512)S(1)} %get-tuple-element.17, f32[4,4096]{1,0:T(4,128)S(1)} %broadcast_divide_fusion), kind=kLoop, calls=%fused_computation.6 | loop fusion | flops 10485248 | bytes 4280320 | tf_op jit(solution)/shard_map/transpose(jvp())/reduce_sum | solution.py:10
  221.3 4.3 %fusion = bf16[512,4096]{1,0:T(8,128)(2,1)} fusion(bf16[512,4096]{1,0:T(8,128)(2,1)S(1)} %copy-done.1, f32[512]{0:T(512)S(1)} %multiply_multiply_fusion, f32[512]{0:T(512)S(1)} %get-tuple-element.13, f32[4096]{0:T(1024)S(1)} %copy-done.7, f32[512]{0:T(512)S(1)} %get-tuple-element.17, f32[4,4096]{1,0:T(4,128)S(1)} %broadcast_divide_fusion), kind=kLoop, calls=%fused_computation.1 | loop fusion | flops 16777216 | bytes 8476672 | tf_op jit(solution)/shard_map/convert_element_type | solution.py:116
  225.6 13.9 %all-to-all-done.3 = f32[16,16,1024]{2,1,0:T(8,128)S(1)} async-done(((f32[16,16,1024]{2,1,0:T(8,128)}), f32[16,16,1024]{2,1,0:T(8,128)S(1)}, u32[]{:S(2)}, u32[]{:S(2)}) %all-to-all-start.3) | async-done | bytes 1048608 | tf_op jit(solution)/shard_map/all_to_all | solution.py:108
  239.4 1.0 copy.21
  (32 shorter events, 0.3 us)
Async XLA Ops:
  7.2 7.2 %copy-start.7 = (f32[4096]{0:T(1024)S(1)}, f32[4096]{0:T(1024)}, u32[]{:S(2)}) copy-start(f32[4096]{0:T(1024)} %param.11) | copy-start | bytes 49156
  7.2 105.7 %all-gather.3.cloned.1.call-start = ((), (), s32[]{:S(2)}) async-start(), calls=%async_computation.4 | async-start | bytes 17825792 | tf_op jit(solution)/shard_map/all_gather | solution.py:46
  9.5 4.9 %copy-start = (bf16[512,4096]{1,0:T(8,128)(2,1)S(1)}, bf16[512,4096]{1,0:T(8,128)(2,1)}, u32[]{:S(2)}) copy-start(bf16[512,4096]{1,0:T(8,128)(2,1)} %param.9) | copy-start | bytes 12582916
  11.2 18.2 %copy-start.10 = (s32[256,1]{0,1:T(1,128)S(1)}, s32[256,1]{0,1:T(1,128)}, u32[]{:S(2)}) copy-start(s32[256,1]{0,1:T(1,128)} %param.12) | copy-start | bytes 3076
  11.2 18.2 %copy-start.9 = (s32[256]{0:T(256)S(1)}, s32[256]{0:T(256)}, u32[]{:S(2)}) copy-start(s32[256]{0:T(256)} %param.13) | copy-start | bytes 3076
  17.5 28.4 %all-to-all-start = ((bf16[16,4,4096]{2,1,0:T(4,128)(2,1)}), bf16[16,4,4096]{2,1,0:T(4,128)(2,1)S(1)}, u32[]{:S(2)}, u32[]{:S(2)}) async-start(bf16[16,4,4096]{2,1,0:T(4,128)(2,1)} %broadcast_in_dim.22), calls=%async_computation | async-start | bytes 1048576 | tf_op jit(solution)/shard_map/all_to_all | solution.py:58
  46.8 80.4 %copy-start.4 = (bf16[256,4096]{1,0:T(8,128)(2,1)}, bf16[256,4096]{1,0:T(8,128)(2,1)S(1)}, u32[]{:S(2)}) copy-start(bf16[256,4096]{1,0:T(8,128)(2,1)S(1)} %convolution_convert_fusion) | copy-start | bytes 6291460
  112.9 9.6 %copy-start.6 = (bf16[256,1024]{1,0:T(8,128)(2,1)S(1)}, bf16[256,1024]{1,0:T(8,128)(2,1)}, u32[]{:S(2)}) copy-start(bf16[256,1024]{1,0:T(8,128)(2,1)} %param.17) | copy-start | bytes 1572868
  112.9 9.6 %copy-start.8 = (f32[4096]{0:T(1024)S(1)}, f32[4096]{0:T(1024)}, u32[]{:S(2)}) copy-start(f32[4096]{0:T(1024)} %param.15) | copy-start | bytes 49156
  122.4 4.8 %copy-start.5 = (bf16[16,256,1024]{2,1,0:T(8,128)(2,1)}, bf16[16,256,1024]{2,1,0:T(8,128)(2,1)S(1)}, u32[]{:S(2)}) copy-start(bf16[16,256,1024]{2,1,0:T(8,128)(2,1)S(1)} %get-tuple-element.10) | copy-start | bytes 25165828
  128.0 1.4 copy-start.2
  130.9 30.0 %all-to-all-start.1 = ((bf16[16,256,256]{2,1,0:T(8,128)(2,1)}), bf16[16,256,256]{2,1,0:T(8,128)(2,1)S(1)}, u32[]{:S(2)}, u32[]{:S(2)}) async-start(bf16[16,256,256]{2,1,0:T(8,128)(2,1)} %bitcast.47), calls=%async_computation.1 | async-start | bytes 4194304 | tf_op jit(solution)/shard_map/all_to_all | solution.py:78
  166.6 44.2 %copy-start.3 = (bf16[256,4096]{1,0:T(8,128)(2,1)S(1)}, bf16[256,4096]{1,0:T(8,128)(2,1)}, u32[]{:S(2)}) copy-start(bf16[256,4096]{1,0:T(8,128)(2,1)} %copy-done.2) | copy-start | bytes 6291460
  206.0 33.5 %all-to-all-start.3 = ((f32[16,16,1024]{2,1,0:T(8,128)}), f32[16,16,1024]{2,1,0:T(8,128)S(1)}, u32[]{:S(2)}, u32[]{:S(2)}) async-start(f32[16,16,1024]{2,1,0:T(8,128)} %broadcast_in_dim.26), calls=%async_computation.3 | async-start | bytes 2097152 | tf_op jit(solution)/shard_map/all_to_all | solution.py:108
  217.3 4.0 %copy-start.1 = (bf16[512,4096]{1,0:T(8,128)(2,1)S(1)}, bf16[512,4096]{1,0:T(8,128)(2,1)}, u32[]{:S(2)}) copy-start(bf16[512,4096]{1,0:T(8,128)(2,1)} %param.9) | copy-start | bytes 12582916
Sparse Core Ops, SparseCore 0:
  10.4 102.4 all-gather.2

commit v5 on v4

--- a/solution.py
+++ b/solution.py
@@ -46,8 +46,6 @@
     gathered = lax.all_gather(
         jnp.concatenate([key_weight, key_grad], axis=0), "fsdp", axis=0, tiled=False
     )
-    weights = gathered[:, :shard_rows].reshape(fsdp_count * shard_rows, key_weight.shape[1])
-    grads_all = gathered[:, shard_rows:].reshape(fsdp_count * key_grad.shape[0], key_grad.shape[1])
     row_count = user_slot.shape[0]
     source = user_source[:, 0]
     seq_count = user_lengths.shape[0]
@@ -74,17 +72,16 @@
 
     scaled, norm_back = jax.vjp(normalize, embedded.astype(jnp.float32))
     hidden = scaled.astype(jnp.bfloat16)
-    hidden_split = hidden.reshape(row_count, fsdp_count, model_width // fsdp_count).transpose(1, 0, 2)
-    hidden_cols = lax.all_to_all(hidden_split, "fsdp", split_axis=0, concat_axis=0, tiled=True).reshape(
-        fsdp_count * row_count, model_width // fsdp_count
-    )
+    hidden_cols = lax.all_to_all(hidden, "fsdp", split_axis=1, concat_axis=0, tiled=True)
+    gathered, hidden_cols = lax.optimization_barrier((gathered, hidden_cols))
+    weights = gathered[:, :shard_rows].reshape(fsdp_count * shard_rows, key_weight.shape[1])
+    grads_all = gathered[:, shard_rows:].reshape(fsdp_count * key_grad.shape[0], key_grad.shape[1])
     key_rows = jnp.dot(hidden, weights, preferred_element_type=jnp.float32).astype(jnp.bfloat16)
     hidden_grad = lax.dot_general(
         key_grad, weights, (((1,), (1,)), ((), ())), preferred_element_type=jnp.float32
     )
     (embed_grad,) = norm_back(hidden_grad)
     pos_grad = jnp.where(alive_mask, embed_grad, jnp.zeros_like(embed_grad)).astype(jnp.bfloat16)
-    hidden_cols, weights, grads_all = lax.optimization_barrier((hidden_cols, weights, grads_all))
     weight_part = lax.dot_general(
         hidden_cols, grads_all, (((0,), (0,)), ((), ())), preferred_element_type=jnp.float32
     )

time: 250 us -> 242 us (0.968)
  blocking collectives: 38 us -> 89.8 us
  waiting for transfers between devices: 117 us -> 65.2 us
  starting transfers between devices: 20.7 us -> 16.1 us
  matrix products: 21.7 us -> 17.6 us
  local copies, waits for them, and re-layouts: 16 us -> 19 us
    all_to_all x0 -> x1, blocking collectives: none -> 52.2 us  [local(): lax.all_to_all(hidden, 'fsdp', split_axis=1, concat_axis=0, tiled=True)]
    all_gather x1, waiting for transfers between devices: 66.1 us -> 34.7 us  [local(): lax.all_gather(jnp.concatenate([key_weight, key_grad], axis=0), 'fsdp', a...]
    all_to_all x1 -> x0, waiting for transfers between devices: 21.1 us -> none  [local(): lax.all_to_all(hidden_split, 'fsdp', split_axis=0, concat_axis=0, tiled=T...]
    all_to_all x1 -> x0, starting transfers between devices: 4.67 us -> none  [local(): lax.all_to_all(hidden_split, 'fsdp', split_axis=0, concat_axis=0, tiled=T...]
    dot_general x0 -> x1, local copies, waits for them, and re-layouts: none -> 4.11 us  [local(): lax.dot_general(hidden_cols, grads_all, (((0,), (0,)), ((), ())), preferr...]
    dot_general x1, matrix products: 3.9 us -> 1.18 us  [local(): lax.dot_general(pick, pos_grad, (((0,), (0,)), ((), ())), preferred_eleme...]
  transfers between devices with their start and end apart: 4 -> 3, of which waited for: 4 -> 3; matrix products, arithmetic and copies ran while one was open for 11% -> 10% of each run, Pallas kernels for 0% -> 0%
where the time goes in v5:
time: 242 us; the launch traced here: 241 us
  blocking collectives  89.8 us (37%)
  waiting for transfers between devices  65.2 us (27%)
  local copies, waits for them, and re-layouts  19 us (8%)
  other arithmetic  18.4 us (8%)
  matrix products  17.6 us (7%)
  starting transfers between devices  16.1 us (7%)
  between operations  14.9 us (6%)
    all_to_all x1, blocking collectives, local(): lax.all_to_all(hidden, 'fsdp', split_axis=1, concat_axis=0, tiled=True)  52.2 us
    all_to_all x1, blocking collectives, local(): lax.all_to_all(outgoing, 'dp', split_axis=0, concat_axis=0, tiled=True)  37.7 us
    all_gather x1, waiting for transfers between devices, local(): lax.all_gather(jnp.concatenate([key_weight, key_grad], axis=0), 'fsdp', a...  34.7 us
    all_to_all x1, waiting for transfers between devices, local(): lax.all_to_all(jnp.broadcast_to(item_emb[None], (group_count, item_count,...  16.5 us
    all_to_all x1, waiting for transfers between devices, local(): lax.all_to_all(jnp.broadcast_to(reduced[None], (group_count,) + reduced.s...  14 us
    all_to_all x1, starting transfers between devices, local(): lax.all_to_all(jnp.broadcast_to(item_emb[None], (group_count, item_count,...  11.2 us
    slice x1, local copies, waits for them, and re-layouts, local(): gathered[:, shard_rows:]  10 us
    dot_general x1, matrix products, local(): jnp.dot(hidden, weights, preferred_element_type=jnp.float32)  6.5 us
  transfers between devices with their start and end apart: 3, of which 3 were waited for; matrix products, arithmetic and copies ran while one was open for 10% of the time, Pallas kernels for 0%

profile of v5, /device:TPU:6, one launch (start us, length us, event | category | flops | bytes accessed | tf_op | source)
XLA Modules:
  0.0 241.0 jit_solution(10942825963424724826)
XLA Ops:
  7.2 2.2 pad_maximum_fusion
  9.5 0.8 convert_element_type.61
  10.3 0.9 fusion.27
  11.2 3.1 %multiply_reduce_fusion.1 = f32[512]{0:T(512)S(1)} fusion(bf16[512,4096]{1,0:T(8,128)(2,1)} %param.9), kind=kLoop, calls=%fused_computation.8 | loop fusion | flops 6290944 | bytes 4196352 | tf_op jit(solution)/shard_map/jvp()/reduce_sum | solution.py:10
  14.4 2.1 multiply_reduce_fusion
  16.5 0.1 divide_convert_fusion
  16.6 1.0 broadcast_in_dim.22
  17.6 11.2 %all-to-all-start = ((bf16[16,4,4096]{2,1,0:T(4,128)(2,1)}), bf16[16,4,4096]{2,1,0:T(4,128)(2,1)S(1)}, u32[]{:S(2)}, u32[]{:S(2)}) async-start(bf16[16,4,4096]{2,1,0:T(4,128)(2,1)} %broadcast_in_dim.22), calls=%async_computation | async-start | bytes 1048576 | tf_op jit(solution)/shard_map/all_to_all | solution.py:56
  29.5 16.5 %all-to-all-done = bf16[16,4,4096]{2,1,0:T(4,128)(2,1)S(1)} async-done(((bf16[16,4,4096]{2,1,0:T(4,128)(2,1)}), bf16[16,4,4096]{2,1,0:T(4,128)(2,1)S(1)}, u32[]{:S(2)}, u32[]{:S(2)}) %all-to-all-start) | async-done | bytes 524320 | tf_op jit(solution)/shard_map/all_to_all | solution.py:56
  45.9 0.1 reshape.141
  46.1 0.8 fusion.8
  46.9 0.6 fusion.10
  47.6 0.7 copy-done.3
  48.2 0.2 copy.22
  48.4 52.2 %all_to_all.34 = bf16[256,16,256]{2,0,1:T(8,128)(2,1)} all-to-all(bf16[256,16,256]{2,0,1:T(8,128)(2,1)S(1)} %bitcast.48), channel_id=1, replica_groups=mesh['dp'=16,'fsdp'=16] {'fsdp'}, dimensions={1} | all-to-all | bytes 4194304 | tf_op jit(solution)/shard_map/all_to_all | solution.py:75
  100.6 34.7 %all-gather.3.cloned.1.call-done = bf16[8192,1024]{1,0:T(8,128)(2,1)} async-done(((bf16[512,1024]{1,0:T(8,128)(2,1)}), bf16[8192,1024]{1,0:T(8,128)(2,1)}) %all-gather.3.cloned.1.call-update) | async-done | bytes 16777232 | tf_op jit(solution)/shard_map/all_gather | solution.py:46
  135.4 4.1 %copy.17 = bf16[256,4096]{1,0:T(8,128)(2,1)} copy(bf16[256,4096]{0,1:T(8,128)(2,1)} %bitcast.47) | data formatting | bytes 4194304 | tf_op jit(solution)/shard_map/dot_general | solution.py:85
  139.5 10.0 %fusion.30 = (bf16[16,256,1024]{2,1,0:T(8,128)(2,1)}, bf16[16,256,1024]{2,1,0:T(8,128)(2,1)S(1)}) fusion(bf16[16,512,1024]{2,1,0:T(8,128)(2,1)} %bitcast.45), kind=kLoop, calls=%fused_computation.55 | loop fusion | bytes 33554432 | tf_op jit(solution)/shard_map/slice | solution.py:78
  149.5 2.7 %fusion.11 = (f32[256]{0:T(256)S(1)}, f32[256,4096]{1,0:T(8,128)S(1)}) fusion(bf16[256,4096]{1,0:T(8,128)(2,1)S(1)} %copy-done.4, f32[4096]{0:T(1024)S(1)} %copy-done.7, bf16[4096,1024]{1,0:T(8,128)(2,1)S(1)} %bitcast.49, bf16[256,1024]{1,0:T(8,128)(2,1)S(1)} %copy-done.5), kind=kOutput, calls=%fused_computation.23 | convolution fusion | flops 2151677696 | bytes 15221760 | tf_op jit(solution)/shard_map/dot_general | solution.py:80
  152.2 0.5 copy-done.2
  152.7 1.2 convolution_convert_fusion.1
  153.9 0.3 reshape.144
  154.2 6.3 %convolution_convert_fusion.2 = bf16[16,16,1024]{2,1,0:T(8,128)(2,1)S(1)} fusion(bf16[16,16,4096]{2,1,0:T(8,128)(2,1)} %bitcast.53, bf16[4096,1024,1]{1,0,2:T(8,128)(2,1)} %bitcast.51), kind=kOutput, calls=%fused_computation.30 | convolution fusion | flops 2147745792 | bytes 11010048 | tf_op jit(solution)/shard_map/dot_general | solution.py:85
  160.7 37.7 %all_to_all.35 = bf16[16,32,1024]{2,1,0:T(8,128)(2,1)S(1)} all-to-all(bf16[16,32,1024]{2,1,0:T(8,128)(2,1)S(1)} %pad_maximum_fusion.1), channel_id=1, replica_groups=mesh['dp'=16,'fsdp'=16] {'dp'}, dimensions={0} | all-to-all | bytes 2097152 | tf_op jit(solution)/shard_map/all_to_all | solution.py:101
  198.3 0.2 convert_reduce_fusion
  198.5 1.1 broadcast_in_dim.26
  199.6 4.8 %all-to-all-start.3 = ((f32[16,16,1024]{2,1,0:T(8,128)}), f32[16,16,1024]{2,1,0:T(8,128)S(1)}, u32[]{:S(2)}, u32[]{:S(2)}) async-start(f32[16,16,1024]{2,1,0:T(8,128)} %broadcast_in_dim.26), calls=%async_computation.3 | async-start | bytes 2097152 | tf_op jit(solution)/shard_map/all_to_all | solution.py:105
  204.4 6.5 %convolution_convert_fusion.3 = bf16[256,1024]{1,0:T(8,128)(2,1)} fusion(bf16[256,4096]{1,0:T(8,128)(2,1)S(1)} %fusion.10, bf16[4096,1024]{1,0:T(8,128)(2,1)} %bitcast.50), kind=kOutput, calls=%fused_computation.31 | convolution fusion | flops 2147745792 | bytes 11010048 | tf_op jit(solution)/shard_map/dot_general | solution.py:79
  211.1 3.9 %fusion.4 = f32[512]{0:T(512)S(1)} fusion(bf16[512,4096]{1,0:T(8,128)(2,1)} %param.9, f32[4096]{0:T(1024)S(1)} %copy-done.6, f32[512]{0:T(512)S(1)} %get-tuple-element.13, f32[4,4096]{1,0:T(4,128)S(1)} %broadcast_divide_fusion), kind=kLoop, calls=%fused_computation.6 | loop fusion | flops 10485248 | bytes 4280320 | tf_op jit(solution)/shard_map/transpose(jvp())/reduce_sum | solution.py:10
  215.0 4.3 %fusion = bf16[512,4096]{1,0:T(8,128)(2,1)} fusion(bf16[512,4096]{1,0:T(8,128)(2,1)S(1)} %copy-done.1, f32[512]{0:T(512)S(1)} %multiply_multiply_fusion, f32[512]{0:T(512)S(1)} %get-tuple-element.11, f32[4096]{0:T(1024)S(1)} %copy-done.6, f32[512]{0:T(512)S(1)} %get-tuple-element.13, f32[4,4096]{1,0:T(4,128)S(1)} %broadcast_divide_fusion), kind=kLoop, calls=%fused_computation.1 | loop fusion | flops 16777216 | bytes 8476672 | tf_op jit(solution)/shard_map/convert_element_type | solution.py:113
  219.2 14.0 %all-to-all-done.3 = f32[16,16,1024]{2,1,0:T(8,128)S(1)} async-done(((f32[16,16,1024]{2,1,0:T(8,128)}), f32[16,16,1024]{2,1,0:T(8,128)S(1)}, u32[]{:S(2)}, u32[]{:S(2)}) %all-to-all-start.3) | async-done | bytes 1048608 | tf_op jit(solution)/shard_map/all_to_all | solution.py:105
  233.2 1.0 copy.25
  (31 shorter events, 0.4 us)
Async XLA Ops:
  7.2 7.2 %copy-start.6 = (f32[4096]{0:T(1024)S(1)}, f32[4096]{0:T(1024)}, u32[]{:S(2)}) copy-start(f32[4096]{0:T(1024)} %param.11) | copy-start | bytes 49156
  7.2 128.2 %all-gather.3.cloned.1.call-start = ((), (), s32[]{:S(2)}) async-start(), calls=%async_computation.4 | async-start | bytes 17825792 | tf_op jit(solution)/shard_map/all_gather | solution.py:46
  9.5 4.9 %copy-start = (bf16[512,4096]{1,0:T(8,128)(2,1)S(1)}, bf16[512,4096]{1,0:T(8,128)(2,1)}, u32[]{:S(2)}) copy-start(bf16[512,4096]{1,0:T(8,128)(2,1)} %param.9) | copy-start | bytes 12582916
  11.2 18.2 %copy-start.9 = (s32[256,1]{0,1:T(1,128)S(1)}, s32[256,1]{0,1:T(1,128)}, u32[]{:S(2)}) copy-start(s32[256,1]{0,1:T(1,128)} %param.12) | copy-start | bytes 3076
  11.2 18.2 %copy-start.8 = (s32[256]{0:T(256)S(1)}, s32[256]{0:T(256)}, u32[]{:S(2)}) copy-start(s32[256]{0:T(256)} %param.13) | copy-start | bytes 3076
  14.3 32.6 %copy-start.7 = (f32[4096]{0:T(1024)S(1)}, f32[4096]{0:T(1024)}, u32[]{:S(2)}) copy-start(f32[4096]{0:T(1024)} %param.15) | copy-start | bytes 49156
  17.6 28.4 %all-to-all-start = ((bf16[16,4,4096]{2,1,0:T(4,128)(2,1)}), bf16[16,4,4096]{2,1,0:T(4,128)(2,1)S(1)}, u32[]{:S(2)}, u32[]{:S(2)}) async-start(bf16[16,4,4096]{2,1,0:T(4,128)(2,1)} %broadcast_in_dim.22), calls=%async_computation | async-start | bytes 1048576 | tf_op jit(solution)/shard_map/all_to_all | solution.py:56
  46.9 1.3 copy-start.3
  139.5 10.0 %copy-start.4 = (bf16[256,4096]{1,0:T(8,128)(2,1)S(1)}, bf16[256,4096]{1,0:T(8,128)(2,1)}, u32[]{:S(2)}) copy-start(bf16[256,4096]{1,0:T(8,128)(2,1)} %copy-done.3) | copy-start | bytes 6291460
  139.5 10.0 %copy-start.5 = (bf16[256,1024]{1,0:T(8,128)(2,1)S(1)}, bf16[256,1024]{1,0:T(8,128)(2,1)}, u32[]{:S(2)}) copy-start(bf16[256,1024]{1,0:T(8,128)(2,1)} %param.17) | copy-start | bytes 1572868
  149.5 3.2 %copy-start.2 = (bf16[16,256,1024]{2,1,0:T(8,128)(2,1)}, bf16[16,256,1024]{2,1,0:T(8,128)(2,1)S(1)}, u32[]{:S(2)}) copy-start(bf16[16,256,1024]{2,1,0:T(8,128)(2,1)S(1)} %get-tuple-element.8) | copy-start | bytes 25165828
  199.6 33.6 %all-to-all-start.3 = ((f32[16,16,1024]{2,1,0:T(8,128)}), f32[16,16,1024]{2,1,0:T(8,128)S(1)}, u32[]{:S(2)}, u32[]{:S(2)}) async-start(f32[16,16,1024]{2,1,0:T(8,128)} %broadcast_in_dim.26), calls=%async_computation.3 | async-start | bytes 2097152 | tf_op jit(solution)/shard_map/all_to_all | solution.py:105
  211.0 4.0 %copy-start.1 = (bf16[512,4096]{1,0:T(8,128)(2,1)S(1)}, bf16[512,4096]{1,0:T(8,128)(2,1)}, u32[]{:S(2)}) copy-start(bf16[512,4096]{1,0:T(8,128)(2,1)} %param.9) | copy-start | bytes 12582916
Sparse Core Ops, SparseCore 0:
  10.4 124.8 all-gather.2

commit v6 on v5

--- a/solution.py
+++ b/solution.py
@@ -74,16 +74,22 @@
     hidden = scaled.astype(jnp.bfloat16)
     hidden_cols = lax.all_to_all(hidden, "fsdp", split_axis=1, concat_axis=0, tiled=True)
     gathered, hidden_cols = lax.optimization_barrier((gathered, hidden_cols))
-    weights = gathered[:, :shard_rows].reshape(fsdp_count * shard_rows, key_weight.shape[1])
-    grads_all = gathered[:, shard_rows:].reshape(fsdp_count * key_grad.shape[0], key_grad.shape[1])
-    key_rows = jnp.dot(hidden, weights, preferred_element_type=jnp.float32).astype(jnp.bfloat16)
+    weights = gathered[:, :shard_rows]
+    grads_all = gathered[:, shard_rows:]
+    hidden_blocks = hidden.reshape(row_count, fsdp_count, shard_rows)
+    key_rows = lax.dot_general(
+        hidden_blocks, weights, (((1, 2), (0, 1)), ((), ())), preferred_element_type=jnp.float32
+    ).astype(jnp.bfloat16)
     hidden_grad = lax.dot_general(
-        key_grad, weights, (((1,), (1,)), ((), ())), preferred_element_type=jnp.float32
-    )
+        key_grad, weights, (((1,), (2,)), ((), ())), preferred_element_type=jnp.float32
+    ).reshape(row_count, model_width)
     (embed_grad,) = norm_back(hidden_grad)
     pos_grad = jnp.where(alive_mask, embed_grad, jnp.zeros_like(embed_grad)).astype(jnp.bfloat16)
     weight_part = lax.dot_general(
-        hidden_cols, grads_all, (((0,), (0,)), ((), ())), preferred_element_type=jnp.float32
+        hidden_cols.reshape(grads_all.shape[0], grads_all.shape[1], shard_rows),
+        grads_all,
+        (((0, 1), (0, 1)), ((), ())),
+        preferred_element_type=jnp.float32,
     )
     weight_rows, weight_cols = weight_part.shape
     item_part = lax.dot_general(

time: 242 us -> 249 us (1.029)
  matrix products: 17.6 us -> 23.5 us
  other arithmetic: 18.4 us -> 23.1 us
  local copies, waits for them, and re-layouts: 19 us -> 15.6 us
    reshape x0 -> x3, local copies, waits for them, and re-layouts: none -> 10.5 us  [the longest x1 5.69 us: local(): hidden_grad = lax.dot_general(key_grad, weights, (((1,), (2,)), ((), ()))...]
    slice x1 -> x0, local copies, waits for them, and re-layouts: 10 us -> none  [local(): gathered[:, shard_rows:]]
    dot_general x3, matrix products: 15.6 us -> 21.5 us  [the longest x1 7.93 us: local(): lax.dot_general(key_grad, weights, (((1,), (2,)), ((), ())), preferred_el...]
    dot_general x1 -> x0, local copies, waits for them, and re-layouts: 4.11 us -> none  [local(): lax.dot_general(hidden_cols, grads_all, (((0,), (0,)), ((), ())), preferr...]
    reduce_sum x1 -> x2, other arithmetic: 3.85 us -> 7.45 us  [rms_scale(): vector * lax.rsqrt(jnp.mean(vector * vector, axis=-1, keepdims=True) + EPS)]
where the time goes in v6:
time: 249 us; the launch traced here: 248 us
  blocking collectives  90 us (36%)
  waiting for transfers between devices  65.3 us (26%)
  matrix products  23.5 us (9%)
  other arithmetic  23.1 us (9%)
  starting transfers between devices  16.1 us (6%)
  local copies, waits for them, and re-layouts  15.6 us (6%)
  between operations  14.9 us (6%)
    all_to_all x1, blocking collectives, local(): lax.all_to_all(hidden, 'fsdp', split_axis=1, concat_axis=0, tiled=True)  52.3 us
    all_to_all x1, blocking collectives, local(): lax.all_to_all(outgoing, 'dp', split_axis=0, concat_axis=0, tiled=True)  37.7 us
    all_gather x1, waiting for transfers between devices, local(): lax.all_gather(jnp.concatenate([key_weight, key_grad], axis=0), 'fsdp', a...  34.8 us
    all_to_all x1, waiting for transfers between devices, local(): lax.all_to_all(jnp.broadcast_to(item_emb[None], (group_count, item_count,...  16.5 us
    all_to_all x1, waiting for transfers between devices, local(): lax.all_to_all(jnp.broadcast_to(reduced[None], (group_count,) + reduced.s...  14 us
    all_to_all x1, starting transfers between devices, local(): lax.all_to_all(jnp.broadcast_to(item_emb[None], (group_count, item_count,...  11.2 us
    dot_general x1, matrix products, local(): lax.dot_general(key_grad, weights, (((1,), (2,)), ((), ())), preferred_el...  7.93 us
    reduce_sum x2, other arithmetic, rms_scale(): vector * lax.rsqrt(jnp.mean(vector * vector, axis=-1, keepdims=True) + EPS)  7.45 us
  transfers between devices with their start and end apart: 3, of which 3 were waited for; matrix products, arithmetic and copies ran while one was open for 10% of the time, Pallas kernels for 0%

profile of v6, /device:TPU:6, one launch (start us, length us, event | category | flops | bytes accessed | tf_op | source)
XLA Modules:
  0.0 248.4 jit_solution(10560789724322854112)
XLA Ops:
  7.2 2.2 pad_maximum_fusion
  9.5 0.8 convert_element_type.61
  10.3 0.9 fusion.47
  11.2 3.1 %multiply_reduce_fusion.1 = f32[512]{0:T(512)S(1)} fusion(bf16[512,4096]{1,0:T(8,128)(2,1)} %param.9), kind=kLoop, calls=%fused_computation.11 | loop fusion | flops 6290944 | bytes 4196352 | tf_op jit(solution)/shard_map/jvp()/reduce_sum | solution.py:10
  14.4 2.1 multiply_reduce_fusion
  16.6 1.0 broadcast_in_dim.22
  17.6 11.2 %all-to-all-start = ((bf16[16,4,4096]{2,1,0:T(4,128)(2,1)}), bf16[16,4,4096]{2,1,0:T(4,128)(2,1)S(1)}, u32[]{:S(2)}, u32[]{:S(2)}) async-start(bf16[16,4,4096]{2,1,0:T(4,128)(2,1)} %broadcast_in_dim.22), calls=%async_computation | async-start | bytes 1048576 | tf_op jit(solution)/shard_map/all_to_all | solution.py:56
  29.5 16.5 %all-to-all-done = bf16[16,4,4096]{2,1,0:T(4,128)(2,1)S(1)} async-done(((bf16[16,4,4096]{2,1,0:T(4,128)(2,1)}), bf16[16,4,4096]{2,1,0:T(4,128)(2,1)S(1)}, u32[]{:S(2)}, u32[]{:S(2)}) %all-to-all-start) | async-done | bytes 524320 | tf_op jit(solution)/shard_map/all_to_all | solution.py:56
  46.1 0.8 fusion.14
  46.9 0.6 fusion.16
  47.6 0.2 copy.30
  47.8 0.4 copy-done.3
  48.2 52.3 %all_to_all.31 = bf16[256,16,256]{2,0,1:T(8,128)(2,1)} all-to-all(bf16[256,16,256]{2,0,1:T(8,128)(2,1)S(1)} %bitcast.61), channel_id=1, replica_groups=mesh['dp'=16,'fsdp'=16] {'fsdp'}, dimensions={1} | all-to-all | bytes 4194304 | tf_op jit(solution)/shard_map/all_to_all | solution.py:75
  100.5 34.8 %all-gather.3.cloned.1.call-done = bf16[8192,1024]{1,0:T(8,128)(2,1)} async-done(((bf16[512,1024]{1,0:T(8,128)(2,1)}), bf16[8192,1024]{1,0:T(8,128)(2,1)}) %all-gather.3.cloned.1.call-update) | async-done | bytes 16777232 | tf_op jit(solution)/shard_map/all_gather | solution.py:46
  135.4 4.6 %copy.16 = bf16[16,256,256]{1,0,2:T(8,128)(2,1)} copy(bf16[16,256,256]{2,1,0:T(8,128)(2,1)} %bitcast.60) | data formatting | bytes 4194304 | tf_op jit(solution)/shard_map/reshape | solution.py:89
  139.9 7.9 %fusion.8 = f32[16,256,256]{2,1,0:T(8,128)} fusion(bf16[16,512,1024]{2,1,0:T(8,128)(2,1)} %bitcast.66, bf16[256,1024]{1,0:T(8,128)(2,1)S(1)} %copy-done.6), kind=kOutput, calls=%fused_computation.12 | convolution fusion | flops 2147483648 | bytes 13107200 | tf_op jit(solution)/shard_map/dot_general | solution.py:83
  147.9 7.0 %fusion.31 = bf16[16,16,1024]{2,1,0:T(8,128)(2,1)} fusion(bf16[16,512,1024]{2,1,0:T(8,128)(2,1)} %bitcast.67, bf16[16,16,16,256]{3,2,1,0:T(8,128)(2,1)S(1)} %bitcast.64), kind=kOutput, calls=%fused_computation.35 | convolution fusion | flops 2147745792 | bytes 11010048 | tf_op jit(solution)/shard_map/dot_general | solution.py:88
  154.9 5.7 %copy.20 = f32[256,4096]{1,0:T(8,128)} copy(f32[256,4096]{0,1:T(8,128)} %bitcast.62) | data formatting | bytes 8388608 | tf_op jit(solution)/shard_map/reshape | solution.py:85
  160.6 3.6 %fusion.17 = f32[256]{0:T(256)S(1)} fusion(bf16[256,4096]{1,0:T(8,128)(2,1)} %copy-done.3, f32[256,4096]{1,0:T(8,128)} %copy.20, f32[4096]{0:T(1024)S(1)} %copy-done.8), kind=kLoop, calls=%fused_computation.28 | loop fusion | flops 4194048 | bytes 6308864 | tf_op jit(solution)/shard_map/transpose(jvp())/reduce_sum | solution.py:10
  164.2 0.4 copy-done.2
  164.6 0.7 copy-done.4
  165.3 1.2 convolution_convert_fusion.1
  166.5 0.3 reshape.148
  166.8 1.1 pad_maximum_fusion.1
  168.0 37.7 %all_to_all.32 = bf16[16,32,1024]{2,1,0:T(8,128)(2,1)S(1)} all-to-all(bf16[16,32,1024]{2,1,0:T(8,128)(2,1)S(1)} %pad_maximum_fusion.1), channel_id=1, replica_groups=mesh['dp'=16,'fsdp'=16] {'dp'}, dimensions={0} | all-to-all | bytes 2097152 | tf_op jit(solution)/shard_map/all_to_all | solution.py:107
  205.9 1.1 broadcast_in_dim.26
  206.9 4.8 %all-to-all-start.3 = ((f32[16,16,1024]{2,1,0:T(8,128)}), f32[16,16,1024]{2,1,0:T(8,128)S(1)}, u32[]{:S(2)}, u32[]{:S(2)}) async-start(f32[16,16,1024]{2,1,0:T(8,128)} %broadcast_in_dim.26), calls=%async_computation.3 | async-start | bytes 2097152 | tf_op jit(solution)/shard_map/all_to_all | solution.py:111
  211.8 6.5 %fusion.28 = bf16[256,1024]{1,0:T(8,128)(2,1)} fusion(bf16[16,512,1024]{2,1,0:T(8,128)(2,1)} %bitcast.68, bf16[32,16,8,256]{3,2,1,0:T(8,128)(2,1)S(1)} %bitcast.59), kind=kOutput, calls=%fused_computation.34 | convolution fusion | flops 2147745792 | bytes 11010048 | tf_op jit(solution)/shard_map/dot_general | solution.py:80
  218.4 3.9 %fusion.4 = f32[512]{0:T(512)S(1)} fusion(bf16[512,4096]{1,0:T(8,128)(2,1)} %param.9, f32[4096]{0:T(1024)S(1)} %copy-done.7, f32[512]{0:T(512)S(1)} %get-tuple-element.11, f32[4,4096]{1,0:T(4,128)S(1)} %broadcast_divide_fusion), kind=kLoop, calls=%fused_computation.6 | loop fusion | flops 10485248 | bytes 4280320 | tf_op jit(solution)/shard_map/transpose(jvp())/reduce_sum | solution.py:10
  222.3 4.3 %fusion = bf16[512,4096]{1,0:T(8,128)(2,1)} fusion(bf16[512,4096]{1,0:T(8,128)(2,1)S(1)} %copy-done.1, f32[512]{0:T(512)S(1)} %multiply_multiply_fusion, f32[512]{0:T(512)S(1)} %get-tuple-element.9, f32[4096]{0:T(1024)S(1)} %copy-done.7, f32[512]{0:T(512)S(1)} %get-tuple-element.11, f32[4,4096]{1,0:T(4,128)S(1)} %broadcast_divide_fusion), kind=kLoop, calls=%fused_computation.1 | loop fusion | flops 16777216 | bytes 8476672 | tf_op jit(solution)/shard_map/convert_element_type | solution.py:119
  226.6 14.0 %all-to-all-done.3 = f32[16,16,1024]{2,1,0:T(8,128)S(1)} async-done(((f32[16,16,1024]{2,1,0:T(8,128)}), f32[16,16,1024]{2,1,0:T(8,128)S(1)}, u32[]{:S(2)}, u32[]{:S(2)}) %all-to-all-start.3) | async-done | bytes 1048608 | tf_op jit(solution)/shard_map/all_to_all | solution.py:111
  240.6 1.0 copy.33
  (34 shorter events, 0.7 us)
Async XLA Ops:
  7.2 7.2 %copy-start.7 = (f32[4096]{0:T(1024)S(1)}, f32[4096]{0:T(1024)}, u32[]{:S(2)}) copy-start(f32[4096]{0:T(1024)} %param.11) | copy-start | bytes 49156
  7.2 128.2 %all-gather.3.cloned.1.call-start = ((), (), s32[]{:S(2)}) async-start(), calls=%async_computation.4 | async-start | bytes 17825792 | tf_op jit(solution)/shard_map/all_gather | solution.py:46
  9.5 4.9 %copy-start = (bf16[512,4096]{1,0:T(8,128)(2,1)S(1)}, bf16[512,4096]{1,0:T(8,128)(2,1)}, u32[]{:S(2)}) copy-start(bf16[512,4096]{1,0:T(8,128)(2,1)} %param.9) | copy-start | bytes 12582916
  11.2 18.2 %copy-start.10 = (s32[256,1]{0,1:T(1,128)S(1)}, s32[256,1]{0,1:T(1,128)}, u32[]{:S(2)}) copy-start(s32[256,1]{0,1:T(1,128)} %param.12) | copy-start | bytes 3076
  11.2 18.2 %copy-start.9 = (s32[256]{0:T(256)S(1)}, s32[256]{0:T(256)}, u32[]{:S(2)}) copy-start(s32[256]{0:T(256)} %param.13) | copy-start | bytes 3076
  14.3 32.6 %copy-start.8 = (f32[4096]{0:T(1024)S(1)}, f32[4096]{0:T(1024)}, u32[]{:S(2)}) copy-start(f32[4096]{0:T(1024)} %param.15) | copy-start | bytes 49156
  17.6 28.4 %all-to-all-start = ((bf16[16,4,4096]{2,1,0:T(4,128)(2,1)}), bf16[16,4,4096]{2,1,0:T(4,128)(2,1)S(1)}, u32[]{:S(2)}, u32[]{:S(2)}) async-start(bf16[16,4,4096]{2,1,0:T(4,128)(2,1)} %broadcast_in_dim.22), calls=%async_computation | async-start | bytes 1048576 | tf_op jit(solution)/shard_map/all_to_all | solution.py:56
  46.9 1.3 copy-start.3
  48.2 91.7 %copy-start.6 = (bf16[256,1024]{1,0:T(8,128)(2,1)S(1)}, bf16[256,1024]{1,0:T(8,128)(2,1)}, u32[]{:S(2)}) copy-start(bf16[256,1024]{1,0:T(8,128)(2,1)} %param.17) | copy-start | bytes 1572868
  139.9 7.9 %copy-start.5 = (bf16[16,256,256]{1,0,2:T(8,128)(2,1)S(1)}, bf16[16,256,256]{1,0,2:T(8,128)(2,1)}, u32[]{:S(2)}) copy-start(bf16[16,256,256]{1,0,2:T(8,128)(2,1)} %copy.16) | copy-start | bytes 6291460
  160.6 4.0 %copy-start.2 = (f32[256,4096]{1,0:T(8,128)S(1)}, f32[256,4096]{1,0:T(8,128)}, u32[]{:S(2)}) copy-start(f32[256,4096]{1,0:T(8,128)} %copy.20) | copy-start | bytes 12582916
  160.6 4.7 %copy-start.4 = (bf16[256,4096]{1,0:T(8,128)(2,1)S(1)}, bf16[256,4096]{1,0:T(8,128)(2,1)}, u32[]{:S(2)}) copy-start(bf16[256,4096]{1,0:T(8,128)(2,1)} %copy-done.3) | copy-start | bytes 6291460
  206.9 33.6 %all-to-all-start.3 = ((f32[16,16,1024]{2,1,0:T(8,128)}), f32[16,16,1024]{2,1,0:T(8,128)S(1)}, u32[]{:S(2)}, u32[]{:S(2)}) async-start(f32[16,16,1024]{2,1,0:T(8,128)} %broadcast_in_dim.26), calls=%async_computation.3 | async-start | bytes 2097152 | tf_op jit(solution)/shard_map/all_to_all | solution.py:111
  218.3 4.0 %copy-start.1 = (bf16[512,4096]{1,0:T(8,128)(2,1)S(1)}, bf16[512,4096]{1,0:T(8,128)(2,1)}, u32[]{:S(2)}) copy-start(bf16[512,4096]{1,0:T(8,128)(2,1)} %param.9) | copy-start | bytes 12582916
Sparse Core Ops, SparseCore 0:
  10.4 124.8 all-gather.2

commit v7 on v5

--- a/solution.py
+++ b/solution.py
@@ -102,13 +102,17 @@
     )
     reduced = arrived[: weight_rows // group_count]
     item_grad = arrived[weight_rows // group_count :].reshape(item_count, model_width)
-    weight_grad = lax.all_to_all(
-        jnp.broadcast_to(reduced[None], (group_count,) + reduced.shape),
-        "dp",
-        split_axis=0,
-        concat_axis=0,
-        tiled=True,
-    ).reshape(weight_rows, weight_cols)
+    weight_grad = (
+        lax.all_to_all(
+            jnp.broadcast_to(reduced.astype(jnp.bfloat16)[None], (group_count,) + reduced.shape),
+            "dp",
+            split_axis=0,
+            concat_axis=0,
+            tiled=True,
+        )
+        .reshape(weight_rows, weight_cols)
+        .astype(jnp.float32)
+    )
     (tokens_back,) = pool_back(item_grad)
     token_grads = tokens_back.reshape(item_count * block_rows, model_width).astype(jnp.bfloat16)
     return (key_rows, weight_grad, token_grads)

time: 242 us -> 231 us (0.955)
  blocking collectives: 89.8 us -> 52.2 us
  waiting for transfers between devices: 65.2 us -> 82.6 us
  starting transfers between devices: 16.1 us -> 24.9 us
    all_to_all x1 -> x0, blocking collectives: 37.7 us -> none  [local(): lax.all_to_all(outgoing, 'dp', split_axis=0, concat_axis=0, tiled=True)]
    all_to_all x1 -> x2, waiting for transfers between devices: 14 us -> 31.4 us  [the longest x1 22.5 us: local(): lax.all_to_all(outgoing, 'dp', split_axis=0, concat_axis=0, tiled=True)]
    all_to_all x1 -> x2, starting transfers between devices: 4.81 us -> 13.6 us  [the longest x1 9.27 us: local(): lax.all_to_all(outgoing, 'dp', split_axis=0, concat_axis=0, tiled=True)]
  transfers between devices with their start and end apart: 3 -> 4, of which waited for: 3 -> 4; matrix products, arithmetic and copies ran while one was open for 10% -> 11% of each run, Pallas kernels for 0% -> 0%
where the time goes in v7:
time: 231 us; the launch traced here: 230 us
  waiting for transfers between devices  82.6 us (36%)
  blocking collectives  52.2 us (23%)
  starting transfers between devices  24.9 us (11%)
  other arithmetic  20.5 us (9%)
  local copies, waits for them, and re-layouts  17.8 us (8%)
  matrix products  17.6 us (8%)
  between operations  14.9 us (6%)
    all_to_all x1, blocking collectives, local(): lax.all_to_all(hidden, 'fsdp', split_axis=1, concat_axis=0, tiled=True)  52.2 us
    all_gather x1, waiting for transfers between devices, local(): lax.all_gather(jnp.concatenate([key_weight, key_grad], axis=0), 'fsdp', a...  34.7 us
    all_to_all x1, waiting for transfers between devices, local(): lax.all_to_all(outgoing, 'dp', split_axis=0, concat_axis=0, tiled=True)  22.5 us
    all_to_all x1, waiting for transfers between devices, local(): lax.all_to_all(jnp.broadcast_to(item_emb[None], (group_count, item_count,...  16.5 us
    all_to_all x1, starting transfers between devices, local(): lax.all_to_all(jnp.broadcast_to(item_emb[None], (group_count, item_count,...  11.2 us
    slice x1, local copies, waits for them, and re-layouts, local(): gathered[:, shard_rows:]  10 us
    all_to_all x1, starting transfers between devices, local(): lax.all_to_all(outgoing, 'dp', split_axis=0, concat_axis=0, tiled=True)  9.27 us
    all_to_all x1, waiting for transfers between devices, local(): lax.all_to_all(jnp.broadcast_to(reduced.astype(jnp.bfloat16)[None], (grou...  8.88 us
  transfers between devices with their start and end apart: 4, of which 4 were waited for; matrix products, arithmetic and copies ran while one was open for 11% of the time, Pallas kernels for 0%

profile of v7, /device:TPU:6, one launch (start us, length us, event | category | flops | bytes accessed | tf_op | source)
XLA Modules:
  0.0 230.5 jit_solution(2943096300493497980)
XLA Ops:
  7.2 2.2 pad_maximum_fusion
  9.5 0.8 convert_element_type.68
  10.3 0.9 fusion.27
  11.2 3.1 %multiply_reduce_fusion.1 = f32[512]{0:T(512)S(1)} fusion(bf16[512,4096]{1,0:T(8,128)(2,1)} %param.9), kind=kLoop, calls=%fused_computation.8 | loop fusion | flops 6290944 | bytes 4196352 | tf_op jit(solution)/shard_map/jvp()/reduce_sum | solution.py:10
  14.4 2.1 multiply_reduce_fusion
  16.6 1.0 broadcast_in_dim.22
  17.6 11.2 %all-to-all-start = ((bf16[16,4,4096]{2,1,0:T(4,128)(2,1)}), bf16[16,4,4096]{2,1,0:T(4,128)(2,1)S(1)}, u32[]{:S(2)}, u32[]{:S(2)}) async-start(bf16[16,4,4096]{2,1,0:T(4,128)(2,1)} %broadcast_in_dim.22), calls=%async_computation | async-start | bytes 1048576 | tf_op jit(solution)/shard_map/all_to_all | solution.py:56
  29.5 16.5 %all-to-all-done = bf16[16,4,4096]{2,1,0:T(4,128)(2,1)S(1)} async-done(((bf16[16,4,4096]{2,1,0:T(4,128)(2,1)}), bf16[16,4,4096]{2,1,0:T(4,128)(2,1)S(1)}, u32[]{:S(2)}, u32[]{:S(2)}) %all-to-all-start) | async-done | bytes 524320 | tf_op jit(solution)/shard_map/all_to_all | solution.py:56
  46.1 0.8 fusion.8
  46.9 0.6 fusion.10
  47.6 0.7 copy-done.3
  48.2 0.2 copy.22
  48.4 52.2 %all_to_all.34 = bf16[256,16,256]{2,0,1:T(8,128)(2,1)} all-to-all(bf16[256,16,256]{2,0,1:T(8,128)(2,1)S(1)} %bitcast.50), channel_id=1, replica_groups=mesh['dp'=16,'fsdp'=16] {'fsdp'}, dimensions={1} | all-to-all | bytes 4194304 | tf_op jit(solution)/shard_map/all_to_all | solution.py:75
  100.6 34.7 %all-gather.3.cloned.1.call-done = bf16[8192,1024]{1,0:T(8,128)(2,1)} async-done(((bf16[512,1024]{1,0:T(8,128)(2,1)}), bf16[8192,1024]{1,0:T(8,128)(2,1)}) %all-gather.3.cloned.1.call-update) | async-done | bytes 16777232 | tf_op jit(solution)/shard_map/all_gather | solution.py:46
  135.4 4.1 %copy.17 = bf16[256,4096]{1,0:T(8,128)(2,1)} copy(bf16[256,4096]{0,1:T(8,128)(2,1)} %bitcast.49) | data formatting | bytes 4194304 | tf_op jit(solution)/shard_map/dot_general | solution.py:85
  139.4 10.0 %fusion.30 = (bf16[16,256,1024]{2,1,0:T(8,128)(2,1)}, bf16[16,256,1024]{2,1,0:T(8,128)(2,1)S(1)}) fusion(bf16[16,512,1024]{2,1,0:T(8,128)(2,1)} %bitcast.47), kind=kLoop, calls=%fused_computation.57 | loop fusion | bytes 33554432 | tf_op jit(solution)/shard_map/slice | solution.py:78
  149.4 2.7 %fusion.11 = (f32[256]{0:T(256)S(1)}, f32[256,4096]{1,0:T(8,128)S(1)}) fusion(bf16[256,4096]{1,0:T(8,128)(2,1)S(1)} %copy-done.4, f32[4096]{0:T(1024)S(1)} %copy-done.7, bf16[4096,1024]{1,0:T(8,128)(2,1)S(1)} %bitcast.51, bf16[256,1024]{1,0:T(8,128)(2,1)S(1)} %copy-done.5), kind=kOutput, calls=%fused_computation.23 | convolution fusion | flops 2151677696 | bytes 15221760 | tf_op jit(solution)/shard_map/dot_general | solution.py:80
  152.2 0.5 copy-done.2
  152.7 1.2 convolution_convert_fusion.1
  153.8 0.3 reshape.144
  154.2 6.3 %convolution_convert_fusion.2 = bf16[16,16,1024]{2,1,0:T(8,128)(2,1)S(1)} fusion(bf16[16,16,4096]{2,1,0:T(8,128)(2,1)} %bitcast.54, bf16[4096,1024,1]{1,0,2:T(8,128)(2,1)} %bitcast.53), kind=kOutput, calls=%fused_computation.30 | convolution fusion | flops 2147745792 | bytes 11010048 | tf_op jit(solution)/shard_map/dot_general | solution.py:85
  160.5 1.1 pad_maximum_fusion.1
  161.6 9.3 %all-to-all-start.2 = ((bf16[16,32,1024]{2,1,0:T(8,128)(2,1)}), bf16[16,32,1024]{2,1,0:T(8,128)(2,1)S(1)}, u32[]{:S(2)}, u32[]{:S(2)}) async-start(bf16[16,32,1024]{2,1,0:T(8,128)(2,1)} %pad_maximum_fusion.1), calls=%async_computation.2 | async-start | bytes 2097152 | tf_op jit(solution)/shard_map/all_to_all | solution.py:101
  170.9 6.5 %convolution_convert_fusion.3 = bf16[256,1024]{1,0:T(8,128)(2,1)} fusion(bf16[256,4096]{1,0:T(8,128)(2,1)S(1)} %fusion.10, bf16[4096,1024]{1,0:T(8,128)(2,1)} %bitcast.52), kind=kOutput, calls=%fused_computation.31 | convolution fusion | flops 2147745792 | bytes 11010048 | tf_op jit(solution)/shard_map/dot_general | solution.py:79
  177.4 22.5 %all-to-all-done.2 = bf16[16,32,1024]{2,1,0:T(8,128)(2,1)S(1)} async-done(((bf16[16,32,1024]{2,1,0:T(8,128)(2,1)}), bf16[16,32,1024]{2,1,0:T(8,128)(2,1)S(1)}, u32[]{:S(2)}, u32[]{:S(2)}) %all-to-all-start.2) | async-done | bytes 1048608 | tf_op jit(solution)/shard_map/all_to_all | solution.py:101
  199.9 0.2 convert_reduce_fusion
  200.2 0.9 broadcast_in_dim.26
  201.0 4.4 %all-to-all-start.3 = ((bf16[16,16,1024]{2,1,0:T(8,128)(2,1)}), bf16[16,16,1024]{2,1,0:T(8,128)(2,1)S(1)}, u32[]{:S(2)}, u32[]{:S(2)}) async-start(bf16[16,16,1024]{2,1,0:T(8,128)(2,1)} %broadcast_in_dim.26), calls=%async_computation.3 | async-start | bytes 1048576 | tf_op jit(solution)/shard_map/all_to_all | solution.py:106
  205.5 3.9 %fusion.4 = f32[512]{0:T(512)S(1)} fusion(bf16[512,4096]{1,0:T(8,128)(2,1)} %param.9, f32[4096]{0:T(1024)S(1)} %copy-done.6, f32[512]{0:T(512)S(1)} %get-tuple-element.11, f32[4,4096]{1,0:T(4,128)S(1)} %broadcast_divide_fusion), kind=kLoop, calls=%fused_computation.6 | loop fusion | flops 10485248 | bytes 4280320 | tf_op jit(solution)/shard_map/transpose(jvp())/reduce_sum | solution.py:10
  209.4 4.3 %fusion = bf16[512,4096]{1,0:T(8,128)(2,1)} fusion(bf16[512,4096]{1,0:T(8,128)(2,1)S(1)} %copy-done.1, f32[512]{0:T(512)S(1)} %multiply_multiply_fusion, f32[512]{0:T(512)S(1)} %get-tuple-element.9, f32[4096]{0:T(1024)S(1)} %copy-done.6, f32[512]{0:T(512)S(1)} %get-tuple-element.11, f32[4,4096]{1,0:T(4,128)S(1)} %broadcast_divide_fusion), kind=kLoop, calls=%fused_computation.1 | loop fusion | flops 16777216 | bytes 8476672 | tf_op jit(solution)/shard_map/convert_element_type | solution.py:117
  213.6 8.9 %all-to-all-done.3 = bf16[16,16,1024]{2,1,0:T(8,128)(2,1)S(1)} async-done(((bf16[16,16,1024]{2,1,0:T(8,128)(2,1)}), bf16[16,16,1024]{2,1,0:T(8,128)(2,1)S(1)}, u32[]{:S(2)}, u32[]{:S(2)}) %all-to-all-start.3) | async-done | bytes 524320 | tf_op jit(solution)/shard_map/all_to_all | solution.py:106
  222.5 1.1 bitcast_convert_fusion
  (33 shorter events, 0.5 us)
Async XLA Ops:
  7.2 7.2 %copy-start.6 = (f32[4096]{0:T(1024)S(1)}, f32[4096]{0:T(1024)}, u32[]{:S(2)}) copy-start(f32[4096]{0:T(1024)} %param.11) | copy-start | bytes 49156
  7.2 128.2 %all-gather.3.cloned.1.call-start = ((), (), s32[]{:S(2)}) async-start(), calls=%async_computation.4 | async-start | bytes 17825792 | tf_op jit(solution)/shard_map/all_gather | solution.py:46
  9.5 4.9 %copy-start = (bf16[512,4096]{1,0:T(8,128)(2,1)S(1)}, bf16[512,4096]{1,0:T(8,128)(2,1)}, u32[]{:S(2)}) copy-start(bf16[512,4096]{1,0:T(8,128)(2,1)} %param.9) | copy-start | bytes 12582916
  11.2 18.2 %copy-start.9 = (s32[256,1]{0,1:T(1,128)S(1)}, s32[256,1]{0,1:T(1,128)}, u32[]{:S(2)}) copy-start(s32[256,1]{0,1:T(1,128)} %param.12) | copy-start | bytes 3076
  11.2 18.2 %copy-start.8 = (s32[256]{0:T(256)S(1)}, s32[256]{0:T(256)}, u32[]{:S(2)}) copy-start(s32[256]{0:T(256)} %param.13) | copy-start | bytes 3076
  14.3 32.6 %copy-start.7 = (f32[4096]{0:T(1024)S(1)}, f32[4096]{0:T(1024)}, u32[]{:S(2)}) copy-start(f32[4096]{0:T(1024)} %param.15) | copy-start | bytes 49156
  17.6 28.4 %all-to-all-start = ((bf16[16,4,4096]{2,1,0:T(4,128)(2,1)}), bf16[16,4,4096]{2,1,0:T(4,128)(2,1)S(1)}, u32[]{:S(2)}, u32[]{:S(2)}) async-start(bf16[16,4,4096]{2,1,0:T(4,128)(2,1)} %broadcast_in_dim.22), calls=%async_computation | async-start | bytes 1048576 | tf_op jit(solution)/shard_map/all_to_all | solution.py:56
  46.9 1.3 copy-start.3
  139.4 10.0 %copy-start.4 = (bf16[256,4096]{1,0:T(8,128)(2,1)S(1)}, bf16[256,4096]{1,0:T(8,128)(2,1)}, u32[]{:S(2)}) copy-start(bf16[256,4096]{1,0:T(8,128)(2,1)} %copy-done.3) | copy-start | bytes 6291460
  139.4 10.0 %copy-start.5 = (bf16[256,1024]{1,0:T(8,128)(2,1)S(1)}, bf16[256,1024]{1,0:T(8,128)(2,1)}, u32[]{:S(2)}) copy-start(bf16[256,1024]{1,0:T(8,128)(2,1)} %param.17) | copy-start | bytes 1572868
  149.4 3.2 %copy-start.2 = (bf16[16,256,1024]{2,1,0:T(8,128)(2,1)}, bf16[16,256,1024]{2,1,0:T(8,128)(2,1)S(1)}, u32[]{:S(2)}) copy-start(bf16[16,256,1024]{2,1,0:T(8,128)(2,1)S(1)} %get-tuple-element.8) | copy-start | bytes 25165828
  161.6 38.3 %all-to-all-start.2 = ((bf16[16,32,1024]{2,1,0:T(8,128)(2,1)}), bf16[16,32,1024]{2,1,0:T(8,128)(2,1)S(1)}, u32[]{:S(2)}, u32[]{:S(2)}) async-start(bf16[16,32,1024]{2,1,0:T(8,128)(2,1)} %pad_maximum_fusion.1), calls=%async_computation.2 | async-start | bytes 2097152 | tf_op jit(solution)/shard_map/all_to_all | solution.py:101
  201.0 21.5 %all-to-all-start.3 = ((bf16[16,16,1024]{2,1,0:T(8,128)(2,1)}), bf16[16,16,1024]{2,1,0:T(8,128)(2,1)S(1)}, u32[]{:S(2)}, u32[]{:S(2)}) async-start(bf16[16,16,1024]{2,1,0:T(8,128)(2,1)} %broadcast_in_dim.26), calls=%async_computation.3 | async-start | bytes 1048576 | tf_op jit(solution)/shard_map/all_to_all | solution.py:106
  205.4 4.0 %copy-start.1 = (bf16[512,4096]{1,0:T(8,128)(2,1)S(1)}, bf16[512,4096]{1,0:T(8,128)(2,1)}, u32[]{:S(2)}) copy-start(bf16[512,4096]{1,0:T(8,128)(2,1)} %param.9) | copy-start | bytes 12582916
Sparse Core Ops, SparseCore 0:
  10.4 124.8 all-gather.2

commit v8 on v7

--- a/solution.py
+++ b/solution.py
@@ -89,19 +89,27 @@
     item_part = lax.dot_general(
         pick, pos_grad, (((0,), (0,)), ((), ())), preferred_element_type=jnp.float32
     )
-    item_rows = item_count * model_width // weight_cols
-    outgoing = jnp.concatenate(
-        [
-            weight_part.reshape(group_count, weight_rows // group_count, weight_cols),
-            item_part.reshape(group_count, item_rows, weight_cols),
-        ],
-        axis=1,
-    ).astype(jnp.bfloat16)
     arrived = jnp.sum(
-        lax.all_to_all(outgoing, "dp", split_axis=0, concat_axis=0, tiled=True).astype(jnp.float32), axis=0
+        lax.all_to_all(
+            weight_part.reshape(group_count, weight_rows // group_count, weight_cols).astype(jnp.bfloat16),
+            "dp",
+            split_axis=0,
+            concat_axis=0,
+            tiled=True,
+        ).astype(jnp.float32),
+        axis=0,
     )
-    reduced = arrived[: weight_rows // group_count]
-    item_grad = arrived[weight_rows // group_count :].reshape(item_count, model_width)
+    reduced = arrived
+    item_grad = jnp.sum(
+        lax.all_to_all(
+            item_part.reshape(group_count, item_count, model_width).astype(jnp.bfloat16),
+            "dp",
+            split_axis=0,
+            concat_axis=0,
+            tiled=True,
+        ).astype(jnp.float32),
+        axis=0,
+    )
     weight_grad = (
         lax.all_to_all(
             jnp.broadcast_to(reduced.astype(jnp.bfloat16)[None], (group_count,) + reduced.shape),

time: 231 us -> 232 us (level)
  starting transfers between devices: 24.9 us -> 30.1 us
  waiting for transfers between devices: 82.6 us -> 78.2 us
    all_to_all x1 -> x2, starting transfers between devices: 9.27 us -> 14.1 us  [the longest x1 9.28 us: local(): lax.all_to_all(weight_part.reshape(group_count, weight_rows // group_coun...]
    dot_general x1, matrix products: 2.73 us -> 6.75 us  [local(): lax.dot_general(key_grad, weights, (((1,), (1,)), ((), ())), preferred_el...]
    all_to_all x1 -> x2, waiting for transfers between devices: 22.5 us -> 18.9 us  [the longest x1 10.5 us: local(): lax.all_to_all(item_part.reshape(group_count, item_count, model_width).as...]
    dot_general x1, matrix products: 6.35 us -> 3.17 us  [local(): lax.dot_general(hidden_cols, grads_all, (((0,), (0,)), ((), ())), preferr...]
  transfers between devices with their start and end apart: 4 -> 5, of which waited for: 4 -> 5; matrix products, arithmetic and copies ran while one was open for 11% -> 15% of each run, Pallas kernels for 0% -> 0%
where the time goes in v8:
time: 232 us; the launch traced here: 231 us
  waiting for transfers between devices  78.2 us (34%)
  blocking collectives  52.2 us (22%)
  starting transfers between devices  30.1 us (13%)
  other arithmetic  19.6 us (8%)
  matrix products  18.4 us (8%)
  local copies, waits for them, and re-layouts  17.6 us (8%)
  between operations  14.9 us (6%)
    all_to_all x1, blocking collectives, local(): lax.all_to_all(hidden, 'fsdp', split_axis=1, concat_axis=0, tiled=True)  52.2 us
    all_gather x1, waiting for transfers between devices, local(): lax.all_gather(jnp.concatenate([key_weight, key_grad], axis=0), 'fsdp', a...  34.7 us
    all_to_all x1, waiting for transfers between devices, local(): lax.all_to_all(jnp.broadcast_to(item_emb[None], (group_count, item_count,...  16.5 us
    all_to_all x1, starting transfers between devices, local(): lax.all_to_all(jnp.broadcast_to(item_emb[None], (group_count, item_count,...  11.2 us
    all_to_all x1, waiting for transfers between devices, local(): lax.all_to_all(item_part.reshape(group_count, item_count, model_width).as...  10.5 us
    slice x1, local copies, waits for them, and re-layouts, local(): gathered[:, shard_rows:]  9.63 us
    all_to_all x1, starting transfers between devices, local(): lax.all_to_all(weight_part.reshape(group_count, weight_rows // group_coun...  9.28 us
    all_to_all x1, waiting for transfers between devices, local(): lax.all_to_all(weight_part.reshape(group_count, weight_rows // group_coun...  8.36 us
  transfers between devices with their start and end apart: 5, of which 5 were waited for; matrix products, arithmetic and copies ran while one was open for 15% of the time, Pallas kernels for 0%

profile of v8, /device:TPU:6, one launch (start us, length us, event | category | flops | bytes accessed | tf_op | source)
XLA Modules:
  0.0 231.1 jit_solution(14766027070340122966)
XLA Ops:
  7.2 2.2 pad_maximum_fusion
  9.5 0.8 convert_element_type.77
  10.3 0.9 fusion.27
  11.2 3.1 %multiply_reduce_fusion.1 = f32[512]{0:T(512)S(1)} fusion(bf16[512,4096]{1,0:T(8,128)(2,1)} %param.9), kind=kLoop, calls=%fused_computation.8 | loop fusion | flops 6290944 | bytes 4196352 | tf_op jit(solution)/shard_map/jvp()/reduce_sum | solution.py:10
  14.4 2.1 multiply_reduce_fusion
  16.6 1.0 broadcast_in_dim.22
  17.6 11.2 %all-to-all-start = ((bf16[16,4,4096]{2,1,0:T(4,128)(2,1)}), bf16[16,4,4096]{2,1,0:T(4,128)(2,1)S(1)}, u32[]{:S(2)}, u32[]{:S(2)}) async-start(bf16[16,4,4096]{2,1,0:T(4,128)(2,1)} %broadcast_in_dim.22), calls=%async_computation | async-start | bytes 1048576 | tf_op jit(solution)/shard_map/all_to_all | solution.py:56
  29.5 16.5 %all-to-all-done = bf16[16,4,4096]{2,1,0:T(4,128)(2,1)S(1)} async-done(((bf16[16,4,4096]{2,1,0:T(4,128)(2,1)}), bf16[16,4,4096]{2,1,0:T(4,128)(2,1)S(1)}, u32[]{:S(2)}, u32[]{:S(2)}) %all-to-all-start) | async-done | bytes 524320 | tf_op jit(solution)/shard_map/all_to_all | solution.py:56
  46.1 0.8 fusion.8
  46.9 0.6 fusion.10
  47.6 0.7 copy-done.2
  48.3 0.2 copy.22
  48.5 52.2 %all_to_all.39 = bf16[256,16,256]{2,0,1:T(8,128)(2,1)} all-to-all(bf16[256,16,256]{2,0,1:T(8,128)(2,1)S(1)} %bitcast.50), channel_id=1, replica_groups=mesh['dp'=16,'fsdp'=16] {'fsdp'}, dimensions={1} | all-to-all | bytes 4194304 | tf_op jit(solution)/shard_map/all_to_all | solution.py:75
  100.7 34.7 %all-gather.3.cloned.1.call-done = bf16[8192,1024]{1,0:T(8,128)(2,1)} async-done(((bf16[512,1024]{1,0:T(8,128)(2,1)}), bf16[8192,1024]{1,0:T(8,128)(2,1)}) %all-gather.3.cloned.1.call-update) | async-done | bytes 16777232 | tf_op jit(solution)/shard_map/all_gather | solution.py:46
  135.4 4.1 %copy.17 = bf16[256,4096]{1,0:T(8,128)(2,1)} copy(bf16[256,4096]{0,1:T(8,128)(2,1)} %bitcast.49) | data formatting | bytes 4194304 | tf_op jit(solution)/shard_map/dot_general | solution.py:85
  139.4 9.6 %fusion.30 = (bf16[16,256,1024]{2,1,0:T(8,128)(2,1)S(1)}, bf16[16,256,1024]{2,1,0:T(8,128)(2,1)}) fusion(bf16[16,512,1024]{2,1,0:T(8,128)(2,1)} %bitcast.47), kind=kLoop, calls=%fused_computation.55 | loop fusion | bytes 33554432 | tf_op jit(solution)/shard_map/slice | solution.py:78
  149.1 3.2 %convolution_convert_fusion.2 = bf16[16,16,1024]{2,1,0:T(8,128)(2,1)} fusion(bf16[16,16,4096]{2,1,0:T(8,128)(2,1)S(1)} %bitcast.54, bf16[4096,1024,1]{1,0,2:T(8,128)(2,1)S(1)} %bitcast.53), kind=kOutput, calls=%fused_computation.29 | convolution fusion | flops 2147745792 | bytes 11010048 | tf_op jit(solution)/shard_map/dot_general | solution.py:85
  152.2 9.3 %all-to-all-start.2 = ((bf16[16,16,1024]{2,1,0:T(8,128)(2,1)}), bf16[16,16,1024]{2,1,0:T(8,128)(2,1)S(1)}, u32[]{:S(2)}, u32[]{:S(2)}) async-start(bf16[16,16,1024]{2,1,0:T(8,128)(2,1)} %convolution_convert_fusion.2), calls=%async_computation.2 | async-start | bytes 1048576 | tf_op jit(solution)/shard_map/all_to_all | solution.py:93
  161.5 6.7 %fusion.11 = (f32[256]{0:T(256)S(1)}, f32[256,4096]{1,0:T(8,128)S(1)}) fusion(bf16[256,4096]{1,0:T(8,128)(2,1)} %copy-done.2, f32[4096]{0:T(1024)S(1)} %copy-done.7, bf16[4096,1024]{1,0:T(8,128)(2,1)} %bitcast.51, bf16[256,1024]{1,0:T(8,128)(2,1)S(1)} %copy-done.5), kind=kOutput, calls=%fused_computation.23 | convolution fusion | flops 2151677696 | bytes 15221760 | tf_op jit(solution)/shard_map/dot_general | solution.py:80
  168.3 1.2 convolution_convert_fusion.1
  169.5 1.0 convert_element_type.88
  170.5 8.4 %all-to-all-done.2 = bf16[16,16,1024]{2,1,0:T(8,128)(2,1)S(1)} async-done(((bf16[16,16,1024]{2,1,0:T(8,128)(2,1)}), bf16[16,16,1024]{2,1,0:T(8,128)(2,1)S(1)}, u32[]{:S(2)}, u32[]{:S(2)}) %all-to-all-start.2) | async-done | bytes 524320 | tf_op jit(solution)/shard_map/all_to_all | solution.py:93
  178.8 4.8 %all-to-all-start.4 = ((bf16[16,4,4096]{2,1,0:T(4,128)(2,1)}), bf16[16,4,4096]{2,1,0:T(4,128)(2,1)S(1)}, u32[]{:S(2)}, u32[]{:S(2)}) async-start(bf16[16,4,4096]{2,1,0:T(4,128)(2,1)} %convert_element_type.88), calls=%async_computation.4 | async-start | bytes 1048576 | tf_op jit(solution)/shard_map/all_to_all | solution.py:104
  183.7 6.5 %convolution_convert_fusion.3 = bf16[256,1024]{1,0:T(8,128)(2,1)} fusion(bf16[256,4096]{1,0:T(8,128)(2,1)S(1)} %fusion.10, bf16[4096,1024]{1,0:T(8,128)(2,1)} %bitcast.52), kind=kOutput, calls=%fused_computation.30 | convolution fusion | flops 2147745792 | bytes 11010048 | tf_op jit(solution)/shard_map/dot_general | solution.py:79
  190.2 10.5 %all-to-all-done.4 = bf16[16,4,4096]{2,1,0:T(4,128)(2,1)S(1)} async-done(((bf16[16,4,4096]{2,1,0:T(4,128)(2,1)}), bf16[16,4,4096]{2,1,0:T(4,128)(2,1)S(1)}, u32[]{:S(2)}, u32[]{:S(2)}) %all-to-all-start.4) | async-done | bytes 524320 | tf_op jit(solution)/shard_map/all_to_all | solution.py:104
  200.8 0.9 broadcast_in_dim.23
  201.6 4.8 %all-to-all-start.3 = ((bf16[16,16,1024]{2,1,0:T(8,128)(2,1)}), bf16[16,16,1024]{2,1,0:T(8,128)(2,1)S(1)}, u32[]{:S(2)}, u32[]{:S(2)}) async-start(bf16[16,16,1024]{2,1,0:T(8,128)(2,1)} %broadcast_in_dim.23), calls=%async_computation.3 | async-start | bytes 1048576 | tf_op jit(solution)/shard_map/all_to_all | solution.py:114
  206.4 0.2 convert_reduce_fusion
  206.7 3.9 %fusion.4 = f32[512]{0:T(512)S(1)} fusion(bf16[512,4096]{1,0:T(8,128)(2,1)} %param.9, f32[4096]{0:T(1024)S(1)} %copy-done.6, f32[512]{0:T(512)S(1)} %get-tuple-element.11, f32[4,4096]{1,0:T(4,128)S(1)} %broadcast_divide_fusion), kind=kLoop, calls=%fused_computation.6 | loop fusion | flops 10485248 | bytes 4280320 | tf_op jit(solution)/shard_map/transpose(jvp())/reduce_sum | solution.py:10
  210.6 4.3 %fusion = bf16[512,4096]{1,0:T(8,128)(2,1)} fusion(bf16[512,4096]{1,0:T(8,128)(2,1)S(1)} %copy-done.1, f32[512]{0:T(512)S(1)} %multiply_multiply_fusion, f32[512]{0:T(512)S(1)} %get-tuple-element.9, f32[4096]{0:T(1024)S(1)} %copy-done.6, f32[512]{0:T(512)S(1)} %get-tuple-element.11, f32[4,4096]{1,0:T(4,128)S(1)} %broadcast_divide_fusion), kind=kLoop, calls=%fused_computation.1 | loop fusion | flops 16777216 | bytes 8476672 | tf_op jit(solution)/shard_map/convert_element_type | solution.py:125
  214.9 8.2 %all-to-all-done.3 = bf16[16,16,1024]{2,1,0:T(8,128)(2,1)S(1)} async-done(((bf16[16,16,1024]{2,1,0:T(8,128)(2,1)}), bf16[16,16,1024]{2,1,0:T(8,128)(2,1)S(1)}, u32[]{:S(2)}, u32[]{:S(2)}) %all-to-all-start.3) | async-done | bytes 524320 | tf_op jit(solution)/shard_map/all_to_all | solution.py:114
  223.1 1.1 bitcast_convert_fusion
  (32 shorter events, 0.5 us)
Async XLA Ops:
  7.2 7.2 %copy-start.6 = (f32[4096]{0:T(1024)S(1)}, f32[4096]{0:T(1024)}, u32[]{:S(2)}) copy-start(f32[4096]{0:T(1024)} %param.11) | copy-start | bytes 49156
  7.2 128.2 %all-gather.3.cloned.1.call-start = ((), (), s32[]{:S(2)}) async-start(), calls=%async_computation.5 | async-start | bytes 17825792 | tf_op jit(solution)/shard_map/all_gather | solution.py:46
  9.5 4.9 %copy-start = (bf16[512,4096]{1,0:T(8,128)(2,1)S(1)}, bf16[512,4096]{1,0:T(8,128)(2,1)}, u32[]{:S(2)}) copy-start(bf16[512,4096]{1,0:T(8,128)(2,1)} %param.9) | copy-start | bytes 12582916
  11.2 18.2 %copy-start.9 = (s32[256,1]{0,1:T(1,128)S(1)}, s32[256,1]{0,1:T(1,128)}, u32[]{:S(2)}) copy-start(s32[256,1]{0,1:T(1,128)} %param.12) | copy-start | bytes 3076
  11.2 18.2 %copy-start.8 = (s32[256]{0:T(256)S(1)}, s32[256]{0:T(256)}, u32[]{:S(2)}) copy-start(s32[256]{0:T(256)} %param.13) | copy-start | bytes 3076
  14.3 32.6 %copy-start.7 = (f32[4096]{0:T(1024)S(1)}, f32[4096]{0:T(1024)}, u32[]{:S(2)}) copy-start(f32[4096]{0:T(1024)} %param.15) | copy-start | bytes 49156
  17.6 28.4 %all-to-all-start = ((bf16[16,4,4096]{2,1,0:T(4,128)(2,1)}), bf16[16,4,4096]{2,1,0:T(4,128)(2,1)S(1)}, u32[]{:S(2)}, u32[]{:S(2)}) async-start(bf16[16,4,4096]{2,1,0:T(4,128)(2,1)} %broadcast_in_dim.22), calls=%async_computation | async-start | bytes 1048576 | tf_op jit(solution)/shard_map/all_to_all | solution.py:56
  46.9 1.4 copy-start.2
  139.4 9.6 %copy-start.4 = (bf16[256,4096]{1,0:T(8,128)(2,1)S(1)}, bf16[256,4096]{1,0:T(8,128)(2,1)}, u32[]{:S(2)}) copy-start(bf16[256,4096]{1,0:T(8,128)(2,1)} %copy.17) | copy-start | bytes 6291460
  149.0 12.5 %copy-start.5 = (bf16[256,1024]{1,0:T(8,128)(2,1)S(1)}, bf16[256,1024]{1,0:T(8,128)(2,1)}, u32[]{:S(2)}) copy-start(bf16[256,1024]{1,0:T(8,128)(2,1)} %param.17) | copy-start | bytes 1572868
  152.2 26.6 %all-to-all-start.2 = ((bf16[16,16,1024]{2,1,0:T(8,128)(2,1)}), bf16[16,16,1024]{2,1,0:T(8,128)(2,1)S(1)}, u32[]{:S(2)}, u32[]{:S(2)}) async-start(bf16[16,16,1024]{2,1,0:T(8,128)(2,1)} %convolution_convert_fusion.2), calls=%async_computation.2 | async-start | bytes 1048576 | tf_op jit(solution)/shard_map/all_to_all | solution.py:93
  161.5 6.8 %copy-start.3 = (bf16[256,4096]{1,0:T(8,128)(2,1)S(1)}, bf16[256,4096]{1,0:T(8,128)(2,1)}, u32[]{:S(2)}) copy-start(bf16[256,4096]{1,0:T(8,128)(2,1)} %copy-done.2) | copy-start | bytes 6291460
  178.8 21.9 %all-to-all-start.4 = ((bf16[16,4,4096]{2,1,0:T(4,128)(2,1)}), bf16[16,4,4096]{2,1,0:T(4,128)(2,1)S(1)}, u32[]{:S(2)}, u32[]{:S(2)}) async-start(bf16[16,4,4096]{2,1,0:T(4,128)(2,1)} %convert_element_type.88), calls=%async_computation.4 | async-start | bytes 1048576 | tf_op jit(solution)/shard_map/all_to_all | solution.py:104
  201.6 21.5 %all-to-all-start.3 = ((bf16[16,16,1024]{2,1,0:T(8,128)(2,1)}), bf16[16,16,1024]{2,1,0:T(8,128)(2,1)S(1)}, u32[]{:S(2)}, u32[]{:S(2)}) async-start(bf16[16,16,1024]{2,1,0:T(8,128)(2,1)} %broadcast_in_dim.23), calls=%async_computation.3 | async-start | bytes 1048576 | tf_op jit(solution)/shard_map/all_to_all | solution.py:114
  206.4 4.2 %copy-start.1 = (bf16[512,4096]{1,0:T(8,128)(2,1)S(1)}, bf16[512,4096]{1,0:T(8,128)(2,1)}, u32[]{:S(2)}) copy-start(bf16[512,4096]{1,0:T(8,128)(2,1)} %param.9) | copy-start | bytes 12582916
Sparse Core Ops, SparseCore 0:
  10.4 124.8 all-gather.2
